TPU v7x, 256 devices: a whole 4x4x8 slice. The times are simulated.
256 devices in a mesh: dp: 16 (over y_hi, x, core), ctx: 16 (over z, y_lo).
Axes of the slice: x: 4, y: 4 (y_hi: 2, y_lo: 2; y = y_hi * 2 + y_lo), z: 8, core: 2. Of those that a mesh axis runs over, the one named last changes fastest.
Arguments:
- queries: bfloat16 [65536, 2048], P(('dp', 'ctx')), parts along dimension 0, may hold values from -6 to 6
- key_states: bfloat16 [65536, 512], P(('dp', 'ctx')), parts along dimension 0, may hold values from -6 to 6
- value_states: bfloat16 [65536, 512], P(('dp', 'ctx')), parts along dimension 0, may hold values from -6 to 6
- grad_output: bfloat16 [65536, 2048], P(('dp', 'ctx')), parts along dimension 0, may hold values from -30 to 30
- log_norms: float32 [16, 65536], P(None, ('dp', 'ctx')), parts along dimension 1, may hold values from 6 to 7.5
- grad_dots: float32 [16, 65536], P(None, ('dp', 'ctx')), parts along dimension 1, may hold values from -150 to 150
- block_routes: int32 [256, 4], P(('dp', 'ctx')), parts along dimension 0, may hold values from 0 to 15, as said below
- owner_steps: int32 [64], P('dp'), parts along dimension 0, may hold values from 0 to 15, as said below
Outputs:
- grad_queries: bfloat16 [65536, 2048], P(('dp', 'ctx')), parts along dimension 0
- grad_keys: bfloat16 [65536, 512], P(('dp', 'ctx')), parts along dimension 0
- grad_values: bfloat16 [65536, 512], P(('dp', 'ctx')), parts along dimension 0
There are 16 independent parts, one for each index of `dp`. A program takes and returns all parts, laid end to end along the dimension named above; each array names one. Nothing has to cross between parts.
Inputs may be any that keep to these rules, and one draw needn't show every extreme that they name: block_routes[b, 0] = b; every entry of row b lies between 0 and b; entries of a row may repeat. `owner_steps`: 4 distinct indices of devices along ctx; device c along ctx holds block c.
All inputs are finite; a program needn't handle non-finite values.
Results may differ from a plain program's by a relative error of at most 0.0065.
Values may be sent and summed in bfloat16 or wider, within the bound.
A program may use at most 128 MiB of HBM per device.

v0:
```python
import math

import jax
import jax.numpy as jnp
from jax import lax
from jax.sharding import PartitionSpec as P

HQ = 16
HK = 4
DH = 128
BLK = 256


def broadcast(value, axis, source):
    kept = jnp.where(lax.axis_index(axis) == source, value, 0).astype(value.dtype)
    return lax.psum(kept, axis)


def pair_terms(query_rows, grad_rows, norm_rows, dot_rows, key_rows, value_rows, allowed):
    rows = query_rows.shape[0]
    cols = key_rows.shape[0]
    group = HQ // HK
    scale = 1.0 / math.sqrt(DH)
    query_heads = query_rows.reshape(rows, HK, group, DH)
    grad_heads = grad_rows.reshape(rows, HK, group, DH)
    key_heads = key_rows.reshape(cols, HK, DH)
    value_heads = value_rows.reshape(cols, HK, DH)
    scores = (
        jnp.einsum("qhgd,khd->hgqk", query_heads, key_heads, preferred_element_type=jnp.float32)
        * scale
    )
    norms = norm_rows.reshape(HK, group, rows, 1)
    dots = dot_rows.reshape(HK, group, rows, 1)
    probs = jnp.where(allowed, jnp.exp(scores - norms), jnp.float32(0.0))
    grad_probs = jnp.einsum(
        "qhgd,khd->hgqk", grad_heads, value_heads, preferred_element_type=jnp.float32
    )
    grad_scores = (probs * (grad_probs - dots)).astype(jnp.bfloat16)
    probs_low = probs.astype(jnp.bfloat16)
    grad_q = (
        jnp.einsum(
            "hgqk,khd->qhgd", grad_scores, key_heads, preferred_element_type=jnp.float32
        ).reshape(rows, HQ * DH)
        * scale
    )
    grad_k = (
        jnp.einsum(
            "hgqk,qhgd->khd", grad_scores, query_heads, preferred_element_type=jnp.float32
        ).reshape(cols, HK * DH)
        * scale
    )
    grad_v = jnp.einsum(
        "hgqk,qhgd->khd", probs_low, grad_heads, preferred_element_type=jnp.float32
    ).reshape(cols, HK * DH)
    return (grad_q, grad_k, grad_v)


def allowed_rows(local_routes, query_start, key_start, tokens, widen, active):
    per_dev = local_routes.shape[0]
    query_blocks = query_start // BLK + jnp.arange(per_dev, dtype=jnp.int32)
    key_blocks = key_start // BLK + jnp.arange(per_dev, dtype=jnp.int32)
    listed = jnp.any(local_routes[:, :, None] == key_blocks[None, None, :], axis=1)
    same = query_blocks[:, None] == key_blocks[None, :]
    chosen = listed & (same | widen) & active
    token_level = jnp.broadcast_to(chosen[:, None, :, None], (per_dev, BLK, per_dev, BLK)).reshape(
        tokens, tokens
    )
    positions = jnp.arange(tokens, dtype=jnp.int32)
    causal = key_start + positions[None, :] <= query_start + positions[:, None]
    return token_level & causal


def on_device(
    queries, key_states, value_states, grad_output, log_norms, grad_dots, block_routes, owner_steps
):
    tokens = queries.shape[0]
    device = lax.axis_index("ctx")
    start = device * tokens
    steps = owner_steps.shape[0]
    is_mine = owner_steps == device
    covered = jnp.any(is_mine)
    local_mask = allowed_rows(block_routes, start, start, tokens, covered, jnp.ones((), jnp.bool_))
    grad_q, grad_k, grad_v = pair_terms(
        queries, grad_output, log_norms, grad_dots, key_states, value_states, local_mask
    )
    for step in range(steps):
        owner = owner_steps[step]
        key_part, value_part = (
            broadcast(key_states, "ctx", owner),
            broadcast(value_states, "ctx", owner),
        )
        step_mask = allowed_rows(
            block_routes, start, owner * tokens, tokens, jnp.ones((), jnp.bool_), owner != device
        )
        term_q, term_k, term_v = pair_terms(
            queries, grad_output, log_norms, grad_dots, key_part, value_part, step_mask
        )
        grad_q = grad_q + term_q
        summed_k, summed_v = lax.psum((term_k, term_v), "ctx")
        taken = owner == device
        grad_k = grad_k + jnp.where(taken, summed_k, jnp.float32(0.0))
        grad_v = grad_v + jnp.where(taken, summed_v, jnp.float32(0.0))
    return (grad_q.astype(jnp.bfloat16), grad_k.astype(jnp.bfloat16), grad_v.astype(jnp.bfloat16))


def solution(mesh):
    return jax.shard_map(
        on_device,
        mesh=mesh,
        in_specs=(
            P(("dp", "ctx"), None),
            P(("dp", "ctx"), None),
            P(("dp", "ctx"), None),
            P(("dp", "ctx"), None),
            P(None, ("dp", "ctx")),
            P(None, ("dp", "ctx")),
            P(("dp", "ctx"), None),
            P("dp"),
        ),
        out_specs=(P(("dp", "ctx"), None), P(("dp", "ctx"), None), P(("dp", "ctx"), None)),
        check_vma=False,
    )
```

profile of v0, /device:TPU:6, one launch (start us, length us, event | category | flops | bytes accessed | tf_op | source)
XLA Modules:
  0.0 442.8 jit_solution(8952580223633291503)
XLA Ops:
  31.8 140.4 %all-reduce.7.cloned.1.call-done = (bf16[256,4,128]{2,0,1:T(8,128)(2,1)}, bf16[256,4,128]{2,0,1:T(8,128)(2,1)}, bf16[256,4,128]{2,0,1:T(8,128)(2,1)}, bf16[256,4...) async-done(((bf16[256,4,128]{2,0,1:T(8,128)(2,1)}, ...) | async-done | bytes 2097168 | tf_op jit(solution)/shard_map/psum | solution.py:16
  173.9 1.9 copy-done.6
  177.8 3.9 fusion.1
  183.3 2.0 copy.116
  186.6 1.8 fusion.27
  188.3 2.7 fusion.5
  191.0 2.1 copy.128
  193.1 3.2 fusion.59
  196.3 2.1 copy.113
  199.6 1.8 fusion.29
  201.4 2.7 fusion.9
  204.1 2.1 copy.125
  206.2 3.2 fusion.58
  209.4 2.0 copy.110
  212.6 1.8 fusion.31
  214.4 2.9 fusion.13
  217.3 2.0 copy.121
  219.3 3.2 fusion.57
  222.6 2.0 copy.106
  235.2 2.1 copy.107
  237.2 3.5 fusion.33
  248.2 183.6 %all-reduce.5.cloned.1.call-done = (f32[256,512]{1,0:T(8,128)}, f32[256,512]{1,0:T(8,128)}, f32[256,512]{1,0:T(8,128)}, f32[256,512]{1,0:T(8,128)}, f32[256,512]...) async-done(((f32[256,512]{1,0:T(8,128)}, f32[256,512]{1,0:T(8,128)}, f32[256,512]{1,0:T(8,128)}, f32[256,512]{1,0:T(8,128)}, ...) | async-done | bytes 4194320 | tf_op jit(solution)/shard_map/psum | solution.py:99
  431.8 2.1 add_convert_fusion.1
  433.9 2.1 add_convert_fusion
  (120 shorter events, 38.4 us)
Async XLA Ops:
  7.2 165.1 %all-reduce.7.cloned.1.call-start = ((), (), s32[]{:S(2)}) async-start(), calls=%async_computation.1 | async-start | bytes 4194304 | tf_op jit(solution)/shard_map/psum | solution.py:16
  13.4 12.2 %copy-start.27 = (f32[16,256]{1,0:T(8,128)S(1)}, f32[16,256]{1,0:T(8,128)}, u32[]{:S(2)}) copy-start(f32[16,256]{1,0:T(8,128)} %param.12) | copy-start | bytes 49156
  13.4 12.2 %copy-start.28 = (f32[16,256]{1,0:T(8,128)S(1)}, f32[16,256]{1,0:T(8,128)}, u32[]{:S(2)}) copy-start(f32[16,256]{1,0:T(8,128)} %param.13) | copy-start | bytes 49156
  13.6 12.1 %copy-start.9 = (bf16[256,2048]{1,0:T(8,128)(2,1)S(1)}, bf16[256,2048]{1,0:T(8,128)(2,1)}, u32[]{:S(2)}) copy-start(bf16[256,2048]{1,0:T(8,128)(2,1)} %param.8) | copy-start | bytes 3145732
  17.0 9.2 %copy-start.10 = (bf16[256,2048]{1,0:T(8,128)(2,1)S(1)}, bf16[256,2048]{1,0:T(8,128)(2,1)}, u32[]{:S(2)}) copy-start(bf16[256,2048]{1,0:T(8,128)(2,1)} %param.11) | copy-start | bytes 3145732
  17.0 9.8 %copy-start.34 = (s32[1,4]{1,0:T(1,128)S(1)}, s32[1,4]{1,0:T(1,128)}, u32[]{:S(2)}) copy-start(s32[1,4]{1,0:T(1,128)} %param.14) | copy-start | bytes 52
  20.4 411.5 %all-reduce.5.cloned.1.call-start = ((), (), s32[]{:S(2)}) async-start(), calls=%async_computation | async-start | bytes 8388608 | tf_op jit(solution)/shard_map/psum | solution.py:99
  25.7 152.2 %copy-start.29 = (f32[4,4,256]{2,1,0:T(4,128)}, f32[4,4,256]{2,1,0:T(4,128)S(1)}, u32[]{:S(2)}) copy-start(f32[4,4,256]{2,1,0:T(4,128)S(1)} %sub.89) | copy-start | bytes 49156
  26.8 150.0 %copy-start.11 = (bf16[256,2048]{0,1:T(8,128)(2,1)}, bf16[256,2048]{0,1:T(8,128)(2,1)S(1)}, u32[]{:S(2)}) copy-start(bf16[256,2048]{0,1:T(8,128)(2,1)S(1)} %copy.188) | copy-start | bytes 3145732
  181.7 3.6 copy-start.21
  186.1 2.3 copy-start.30
  186.1 2.3 copy-start.37
  191.0 7.3 %copy-start.19 = (bf16[256,4,128]{2,0,1:T(8,128)(2,1)S(1)}, bf16[256,4,128]{2,0,1:T(8,128)(2,1)}, u32[]{:S(2)}) copy-start(bf16[256,4,128]{2,0,1:T(8,128)(2,1)} %get-tuple-element.26) | copy-start | bytes 786436
  199.1 2.3 copy-start.31
  199.1 2.3 copy-start.36
  204.1 7.3 %copy-start.17 = (bf16[256,4,128]{2,0,1:T(8,128)(2,1)S(1)}, bf16[256,4,128]{2,0,1:T(8,128)(2,1)}, u32[]{:S(2)}) copy-start(bf16[256,4,128]{2,0,1:T(8,128)(2,1)} %get-tuple-element.28) | copy-start | bytes 786436
  212.1 2.3 copy-start.32
  212.1 2.3 copy-start.35
  219.3 7.9 %copy-start.16 = (bf16[256,512]{1,0:T(8,128)(2,1)S(1)}, bf16[256,512]{1,0:T(8,128)(2,1)}, u32[]{:S(2)}) copy-start(bf16[256,512]{1,0:T(8,128)(2,1)} %param.9) | copy-start | bytes 786436
  224.6 7.0 %copy-start.33 = (f32[4,4,256]{2,1,0:T(4,128)S(1)}, f32[4,4,256]{2,1,0:T(4,128)}, u32[]{:S(2)}) copy-start(f32[4,4,256]{2,1,0:T(4,128)} %copy-done.29) | copy-start | bytes 49156
  237.2 4.5 %copy-start.23 = (bf16[256,4,128]{2,0,1:T(8,128)(2,1)S(1)}, bf16[256,4,128]{2,0,1:T(8,128)(2,1)}, u32[]{:S(2)}) copy-start(bf16[256,4,128]{2,0,1:T(8,128)(2,1)} %get-tuple-element.22) | copy-start | bytes 786436
  241.7 2.3 copy-start.20
  245.7 186.1 %copy-start.8 = (f32[256,512]{1,0:T(8,128)S(1)}, f32[256,512]{1,0:T(8,128)}, u32[]{:S(2)}) copy-start(f32[256,512]{1,0:T(8,128)} %copy.107) | copy-start | bytes 1572868
  246.8 187.1 %copy-start.7 = (f32[256,512]{1,0:T(8,128)S(1)}, f32[256,512]{1,0:T(8,128)}, u32[]{:S(2)}) copy-start(f32[256,512]{1,0:T(8,128)} %copy.122) | copy-start | bytes 1572868
  (16 other events, 24.9 us)
Sparse Core Ops, SparseCore 0:
  20.5 151.6 all-reduce.6
  224.7 207.0 all-reduce.4
where the time goes:
time: 444 us; the launch traced here: 443 us
  waiting for transfers between devices  324 us (73%)
  matrix products  43.5 us (10%)
  local copies, waits for them, and re-layouts  41.1 us (9%)
  between operations  27.4 us (6%)
  other arithmetic  6.7 us (2%)
    psum x1, waiting for transfers between devices, on_device(): summed_k, summed_v = lax.psum((term_k, term_v), 'ctx')  184 us
    psum x1, waiting for transfers between devices, broadcast(): return lax.psum(kept, axis)  140 us
    dot_general x5, matrix products, pair_terms(): jnp.einsum('qhgd,khd->hgqk', grad_heads, value_heads, preferred_element_t...  13.5 us
    dot_general x5, matrix products, pair_terms(): jnp.einsum('hgqk,qhgd->khd', grad_scores, query_heads, preferred_element_...  12.8 us
    mul x5, local copies, waits for them, and re-layouts, pair_terms(): jnp.einsum('hgqk,qhgd->khd', grad_scores, query_heads, preferred_element_...  10.2 us
    unnamed x79, local copies, waits for them, and re-layouts  9.8 us
    dot_general x5, matrix products, pair_terms(): jnp.einsum('hgqk,qhgd->khd', probs_low, grad_heads, preferred_element_typ...  9.73 us
  transfers between devices with their start and end apart: 2, of which 2 were waited for; matrix products, arithmetic and copies ran while one was open for 5% of the time, Pallas kernels for 0%

commit v1 on v0

--- a/solution.py
+++ b/solution.py
@@ -1,19 +1,119 @@
+import functools
 import math
 
 import jax
 import jax.numpy as jnp
 from jax import lax
+from jax.experimental import pallas as pl
+from jax.experimental.pallas import tpu as pltpu
 from jax.sharding import PartitionSpec as P
 
 HQ = 16
 HK = 4
 DH = 128
 BLK = 256
-
-
-def broadcast(value, axis, source):
-    kept = jnp.where(lax.axis_index(axis) == source, value, 0).astype(value.dtype)
-    return lax.psum(kept, axis)
+MESH = pl.DeviceIdType.MESH
+
+
+def ring_pos(c, n):
+    y = c % 2
+    z = c // 2
+    return (1 - y) * z + y * (n - 1 - z)
+
+
+def ring_ctx(p, n):
+    q = p // (n // 2)
+    return (1 - q) * (2 * p) + q * (2 * (n - 1 - p) + 1)
+
+
+def ring_kernel(n, x_ref, o_ref, rbuf, rs_send, rs_recv, ag_send, ag_recv):
+    me = lax.axis_index("ctx")
+    row = lax.axis_index("dp")
+    pos = ring_pos(me, n)
+    right = ring_ctx((pos + 1) % n, n)
+    left = ring_ctx((pos + n - 1) % n, n)
+    peers = (right, left)
+
+    barrier = pltpu.get_barrier_semaphore()
+    for nb in (left, right):
+        pl.semaphore_signal(barrier, inc=1, device_id=(row, nb), device_id_type=MESH)
+    pl.semaphore_wait(barrier, 2)
+
+    o_ref[...] = x_ref[...]
+
+    def rs_copy(d, s):
+        send = (pos + n - s) % n if d == 0 else (pos + s) % n
+        return pltpu.make_async_remote_copy(
+            src_ref=o_ref.at[d, send],
+            dst_ref=rbuf.at[d, s],
+            send_sem=rs_send.at[d, s],
+            recv_sem=rs_recv.at[d, s],
+            device_id=(row, peers[d]),
+            device_id_type=MESH,
+        )
+
+    def rs_step(s, carry):
+        copies = [rs_copy(d, s) for d in range(2)]
+        for c in copies:
+            c.start()
+        for d in range(2):
+            copies[d].wait_recv()
+            got = (pos + 2 * n - s - 1) % n if d == 0 else (pos + s + 1) % n
+            o_ref[d, got] = o_ref[d, got] + rbuf[d, s]
+        for c in copies:
+            c.wait_send()
+        return carry
+
+    lax.fori_loop(0, n - 1, rs_step, 0)
+
+    def ag_copy(d, t):
+        chunk = (pos + 1 + n - t) % n if d == 0 else (pos + n - 1 + t) % n
+        return pltpu.make_async_remote_copy(
+            src_ref=o_ref.at[d, chunk],
+            dst_ref=o_ref.at[d, chunk],
+            send_sem=ag_send.at[d, t],
+            recv_sem=ag_recv.at[d, t],
+            device_id=(row, peers[d]),
+            device_id_type=MESH,
+        )
+
+    def ag_step(t, carry):
+        copies = [ag_copy(d, t) for d in range(2)]
+        for c in copies:
+            c.start()
+        for c in copies:
+            c.wait_recv()
+        for c in copies:
+            c.wait_send()
+        return carry
+
+    lax.fori_loop(0, n - 1, ag_step, 0)
+
+
+def ring_allreduce(x, n, cid):
+    _, _, rows, cols = x.shape
+    return pl.pallas_call(
+        functools.partial(ring_kernel, n),
+        out_shape=jax.ShapeDtypeStruct(x.shape, x.dtype),
+        in_specs=[pl.BlockSpec(memory_space=pltpu.VMEM)],
+        out_specs=pl.BlockSpec(memory_space=pltpu.VMEM),
+        scratch_shapes=[
+            pltpu.VMEM((2, n - 1, rows, cols), x.dtype),
+            pltpu.SemaphoreType.DMA((2, n - 1)),
+            pltpu.SemaphoreType.DMA((2, n - 1)),
+            pltpu.SemaphoreType.DMA((2, n - 1)),
+            pltpu.SemaphoreType.DMA((2, n - 1)),
+        ],
+        compiler_params=pltpu.CompilerParams(collective_id=cid, has_side_effects=True),
+    )(x)
+
+
+def slot_allreduce(slots, n, cid):
+    steps, rows, cols = slots.shape
+    total = steps * rows
+    chunk = total // (2 * n)
+    out = ring_allreduce(slots.reshape(2, n, chunk, cols), n, cid)
+    return out.reshape(steps, rows, cols)
 
 
 def pair_terms(query_rows, grad_rows, norm_rows, dot_rows, key_rows, value_rows, allowed):
@@ -70,42 +170,51 @@
     return token_level & causal
 
 
-def on_device(
-    queries, key_states, value_states, grad_output, log_norms, grad_dots, block_routes, owner_steps
-):
-    tokens = queries.shape[0]
-    device = lax.axis_index("ctx")
-    start = device * tokens
-    steps = owner_steps.shape[0]
-    is_mine = owner_steps == device
-    covered = jnp.any(is_mine)
-    local_mask = allowed_rows(block_routes, start, start, tokens, covered, jnp.ones((), jnp.bool_))
-    grad_q, grad_k, grad_v = pair_terms(
-        queries, grad_output, log_norms, grad_dots, key_states, value_states, local_mask
-    )
-    for step in range(steps):
-        owner = owner_steps[step]
-        key_part, value_part = (
-            broadcast(key_states, "ctx", owner),
-            broadcast(value_states, "ctx", owner),
+def make_on_device(n):
+    def on_device(
+        queries, key_states, value_states, grad_output, log_norms, grad_dots, block_routes, owner_steps
+    ):
+        tokens = queries.shape[0]
+        features = key_states.shape[1]
+        device = lax.axis_index("ctx")
+        start = device * tokens
+        steps = owner_steps.shape[0]
+        is_mine = owner_steps == device
+        covered = jnp.any(is_mine)
+        kv = jnp.concatenate([key_states, value_states], axis=1)
+        kv_slots = jnp.where(is_mine[:, None, None], kv[None], jnp.zeros((), kv.dtype))
+        kv_all = slot_allreduce(kv_slots, n, 0)
+        local_mask = allowed_rows(block_routes, start, start, tokens, covered, jnp.ones((), jnp.bool_))
+        grad_q, grad_k, grad_v = pair_terms(
+            queries, grad_output, log_norms, grad_dots, key_states, value_states, local_mask
         )
-        step_mask = allowed_rows(
-            block_routes, start, owner * tokens, tokens, jnp.ones((), jnp.bool_), owner != device
-        )
-        term_q, term_k, term_v = pair_terms(
-            queries, grad_output, log_norms, grad_dots, key_part, value_part, step_mask
-        )
-        grad_q = grad_q + term_q
-        summed_k, summed_v = lax.psum((term_k, term_v), "ctx")
-        taken = owner == device
-        grad_k = grad_k + jnp.where(taken, summed_k, jnp.float32(0.0))
-        grad_v = grad_v + jnp.where(taken, summed_v, jnp.float32(0.0))
-    return (grad_q.astype(jnp.bfloat16), grad_k.astype(jnp.bfloat16), grad_v.astype(jnp.bfloat16))
+        terms = []
+        for step in range(steps):
+            owner = owner_steps[step]
+            key_part = kv_all[step, :, :features]
+            value_part = kv_all[step, :, features:]
+            step_mask = allowed_rows(
+                block_routes, start, owner * tokens, tokens, jnp.ones((), jnp.bool_), owner != device
+            )
+            term_q, term_k, term_v = pair_terms(
+                queries, grad_output, log_norms, grad_dots, key_part, value_part, step_mask
+            )
+            grad_q = grad_q + term_q
+            terms.append(jnp.concatenate([term_k, term_v], axis=1))
+        summed = slot_allreduce(jnp.stack(terms), n, 1)
+        for step in range(steps):
+            taken = is_mine[step]
+            grad_k = grad_k + jnp.where(taken, summed[step, :, :features], jnp.float32(0.0))
+            grad_v = grad_v + jnp.where(taken, summed[step, :, features:], jnp.float32(0.0))
+        return (grad_q.astype(jnp.bfloat16), grad_k.astype(jnp.bfloat16), grad_v.astype(jnp.bfloat16))
+
+    return on_device
 
 
 def solution(mesh):
+    n = mesh.shape["ctx"]
     return jax.shard_map(
-        on_device,
+        make_on_device(n),
         mesh=mesh,
         in_specs=(
             P(("dp", "ctx"), None),

time: 444 us -> 395 us (0.89)
  waiting for transfers between devices: 324 us -> 0 us
  Pallas kernels: 0 us -> 283 us
  between operations: 27.4 us -> 9.01 us
  other arithmetic: 6.7 us -> 24.3 us
  local copies, waits for them, and re-layouts: 41.1 us -> 35.9 us
    psum x2 -> x0, waiting for transfers between devices: 324 us -> none  [the longest x1 184 us: on_device(): summed_k, summed_v = lax.psum((term_k, term_v), 'ctx')]
    pallas_call x0 -> x2, Pallas kernels: none -> 283 us  [ring_allreduce(): pl.pallas_call(functools.partial(ring_kernel, n), out_shape=jax.ShapeDtyp...]
    another operation x0 -> x5, other arithmetic: none -> 11.9 us  [on_device(): summed = slot_allreduce(jnp.stack(terms), n, 1)]
    dot_general x5, matrix products: 2.96 us -> 12 us  [pair_terms(): jnp.einsum('hgqk,khd->qhgd', grad_scores, key_heads, preferred_element_ty...]
    dot_general x5, matrix products: 13.5 us -> 7.12 us  [pair_terms(): jnp.einsum('qhgd,khd->hgqk', grad_heads, value_heads, preferred_element_t...]
    dot_general x5, matrix products: 12.8 us -> 7.38 us  [pair_terms(): jnp.einsum('hgqk,qhgd->khd', grad_scores, query_heads, preferred_element_...]
    mul x5, local copies, waits for them, and re-layouts: 10.2 us -> 5.41 us  [pair_terms(): jnp.einsum('hgqk,qhgd->khd', grad_scores, query_heads, preferred_element_...]
    unnamed x79 -> x71, local copies, waits for them, and re-layouts: 9.8 us -> 10.2 us
  transfers between devices with their start and end apart: 2 -> 0, of which waited for: 2 -> 0; matrix products, arithmetic and copies ran while one was open for 5% -> 0% of each run, Pallas kernels for 0% -> 0%
where the time goes in v1:
time: 395 us; the launch traced here: 393 us
  Pallas kernels  283 us (72%)
  matrix products  41.2 us (10%)
  local copies, waits for them, and re-layouts  35.9 us (9%)
  other arithmetic  24.3 us (6%)
  between operations  9.01 us (2%)
    pallas_call x2, Pallas kernels, ring_allreduce(): pl.pallas_call(functools.partial(ring_kernel, n), out_shape=jax.ShapeDtyp...  283 us
    dot_general x5, matrix products, pair_terms(): jnp.einsum('hgqk,khd->qhgd', grad_scores, key_heads, preferred_element_ty...  12 us
    another operation x5, other arithmetic, on_device(): summed = slot_allreduce(jnp.stack(terms), n, 1)  11.9 us
    unnamed x71, local copies, waits for them, and re-layouts  10.2 us
    reshape x5, local copies, waits for them, and re-layouts, pair_terms(): grad_v = jnp.einsum('hgqk,qhgd->khd', probs_low, grad_heads, preferred_el...  8.36 us
    dot_general x5, matrix products, pair_terms(): jnp.einsum('hgqk,qhgd->khd', probs_low, grad_heads, preferred_element_typ...  8.08 us

profile of v1, /device:TPU:6, one launch (start us, length us, event | category | flops | bytes accessed | tf_op | source)
XLA Modules:
  0.0 393.3 jit_solution(5677899160118008714)
XLA Ops:
  16.3 1.7 reshape.244
  25.3 127.8 %shard_map.103 = bf16[2,16,32,1024]{3,2,1,0:T(8,128)(2,1)} custom-call(bf16[2,16,32,1024]{3,2,1,0:T(8,128)(2,1)} %broadcast_select_fusion.x_ref), custom_call_target="tpu_custom_call" | custom-call | tf_op jit(solution)/shard_map/pallas_call | solution.py:95
  153.1 1.7 fusion.90
  161.8 1.8 fusion.31
  165.0 2.0 copy.105
  168.7 2.8 fusion.95
  172.8 2.1 maximum_bitcast_fusion
  174.9 1.7 fusion.96
  176.7 1.8 fusion.29
  179.9 2.0 copy.111
  183.6 2.8 fusion.97
  187.7 2.1 maximum_bitcast_fusion.1
  189.8 1.7 fusion.98
  191.5 1.8 fusion.27
  194.8 2.0 copy.117
  196.8 1.8 fusion.59
  198.6 2.7 fusion.99
  202.7 2.1 maximum_bitcast_fusion.2
  206.5 1.8 fusion.25
  209.8 2.0 copy.123
  213.4 2.7 fusion.101
  218.5 4.4 %pad_maximum_fusion = f32[4,256,1024]{2,1,0:T(8,128)} fusion(f32[1,256,1024]{2,1,0:T(8,128)S(1)} %maximum_bitcast_fusion.3, f32[1,256,1024]{2,1,0:T(8,128)} %maximum_bitcast_fusion.2, f32[1,256,1024]{2,1,0:T(8,128)} %maximum_bitcast_fusion.1, f32[1,256,1024]{2,1,0:T(8,128)} %maximum_bitcast_fusion), kind=kLoop, calls=%fused_computation | loop fusion | flops 3145728 | bytes 8388608 | tf_op jit(solution)/shard_map/stack | solution.py:204
  222.9 155.0 %shard_map.104 = f32[2,16,32,1024]{3,2,1,0:T(8,128)} custom-call(f32[2,16,32,1024]{3,2,1,0:T(8,128)} %bitcast.354), custom_call_target="tpu_custom_call" | custom-call | tf_op jit(solution)/shard_map/pallas_call | solution.py:95
  387.3 6.0 %fusion.63 = (bf16[256,512]{1,0:T(8,128)(2,1)}, bf16[256,512]{1,0:T(8,128)(2,1)}) fusion(f32[4,256,1024]{2,1,0:T(8,128)} %bitcast.353, f32[256,512]{1,0:T(8,128)S(1)} %copy.127, pred[]{:T(512)} %bitcast.97, pred[]{:T(512)} %bitcast.95, pred[]{:T(512)} %bitcast.93, pred[]{:T(512)} %bitcast.53, f32[256,512]{1,0:T(8,128)S(1)} %copy.124), kind=kLoop, calls=%fused_computation.84 | loop fusion | flops 2359296 | bytes 5767172 | tf_op jit(solution)/shard_map/convert_element_type | solution.py:209
  (112 shorter events, 49.8 us)
Async XLA Ops:
  0.6 21.5 %copy-start.5 = (bf16[256,2048]{1,0:T(8,128)(2,1)S(1)}, bf16[256,2048]{1,0:T(8,128)(2,1)}, u32[]{:S(2)}) copy-start(bf16[256,2048]{1,0:T(8,128)(2,1)} %param.11) | copy-start | bytes 3145732
  158.3 3.4 copy-start.6
  159.1 2.6 copy-start.24
  161.7 1.8 copy-start.7
  161.7 1.8 copy-start.19
  161.7 1.8 copy-start.25
  161.7 1.8 copy-start.26
  171.5 5.2 %copy-start.8 = (bf16[256,2048]{0,1:T(8,128)(2,1)S(1)}, bf16[256,2048]{0,1:T(8,128)(2,1)}, u32[]{:S(2)}) copy-start(bf16[256,2048]{0,1:T(8,128)(2,1)} %copy.200) | copy-start | bytes 3145732
  171.5 5.2 %copy-start.22 = (pred[256,256]{0,1:T(8,128)(4,1)S(1)}, pred[256,256]{0,1:T(8,128)(4,1)}, u32[]{:S(2)}) copy-start(pred[256,256]{0,1:T(8,128)(4,1)} %get-tuple-element.25) | copy-start | bytes 196612
  176.7 1.8 copy-start.9
  176.7 1.8 copy-start.18
  176.7 1.8 copy-start.23
  186.3 5.2 %copy-start.10 = (bf16[256,2048]{0,1:T(8,128)(2,1)S(1)}, bf16[256,2048]{0,1:T(8,128)(2,1)}, u32[]{:S(2)}) copy-start(bf16[256,2048]{0,1:T(8,128)(2,1)} %copy.200) | copy-start | bytes 3145732
  186.3 5.2 %copy-start.20 = (pred[256,256]{0,1:T(8,128)(4,1)S(1)}, pred[256,256]{0,1:T(8,128)(4,1)}, u32[]{:S(2)}) copy-start(pred[256,256]{0,1:T(8,128)(4,1)} %get-tuple-element.26) | copy-start | bytes 196612
  191.5 1.8 copy-start.11
  191.5 1.8 copy-start.17
  191.5 1.8 copy-start.21
  191.5 1.8 copy-start.28
  201.3 5.2 %copy-start.12 = (bf16[256,2048]{0,1:T(8,128)(2,1)S(1)}, bf16[256,2048]{0,1:T(8,128)(2,1)}, u32[]{:S(2)}) copy-start(bf16[256,2048]{0,1:T(8,128)(2,1)} %copy.200) | copy-start | bytes 3145732
  206.5 1.8 copy-start.13
  206.5 1.8 copy-start.16
  380.1 2.2 copy-start.1
  380.1 2.8 copy-start.2
  380.1 3.4 copy-start.3
  (7 other events, 10.0 us)

commit v2 on v1

--- a/solution.py
+++ b/solution.py
@@ -15,94 +15,83 @@
 MESH = pl.DeviceIdType.MESH
 
 
-def ring_pos(c, n):
-    y = c % 2
-    z = c // 2
-    return (1 - y) * z + y * (n - 1 - z)
-
-
-def ring_ctx(p, n):
-    q = p // (n // 2)
-    return (1 - q) * (2 * p) + q * (2 * (n - 1 - p) + 1)
-
-
-def ring_kernel(n, x_ref, o_ref, rbuf, rs_send, rs_recv, ag_send, ag_recv):
+def direct_kernel(n, x_ref, o_ref, rbuf, rs_send, rs_recv, ag_send, ag_recv):
     me = lax.axis_index("ctx")
     row = lax.axis_index("dp")
-    pos = ring_pos(me, n)
-    right = ring_ctx((pos + 1) % n, n)
-    left = ring_ctx((pos + n - 1) % n, n)
-    peers = (right, left)
+    peers = [(me + k) % n for k in range(1, n)]
 
     barrier = pltpu.get_barrier_semaphore()
-    for nb in (left, right):
+    for nb in peers:
         pl.semaphore_signal(barrier, inc=1, device_id=(row, nb), device_id_type=MESH)
-    pl.semaphore_wait(barrier, 2)
-
-    o_ref[...] = x_ref[...]
-
-    def rs_copy(d, s):
-        send = (pos + n - s) % n if d == 0 else (pos + s) % n
+    pl.semaphore_wait(barrier, n - 1)
+
+    def rs_copy(nb):
         return pltpu.make_async_remote_copy(
-            src_ref=o_ref.at[d, send],
-            dst_ref=rbuf.at[d, s],
-            send_sem=rs_send.at[d, s],
-            recv_sem=rs_recv.at[d, s],
-            device_id=(row, peers[d]),
+            src_ref=x_ref.at[nb],
+            dst_ref=rbuf.at[me],
+            send_sem=rs_send.at[nb],
+            recv_sem=rs_recv.at[me],
+            device_id=(row, nb),
             device_id_type=MESH,
         )
 
-    def rs_step(s, carry):
-        copies = [rs_copy(d, s) for d in range(2)]
-        for c in copies:
-            c.start()
-        for d in range(2):
-            copies[d].wait_recv()
-            got = (pos + 2 * n - s - 1) % n if d == 0 else (pos + s + 1) % n
-            o_ref[d, got] = o_ref[d, got] + rbuf[d, s]
-        for c in copies:
-            c.wait_send()
-        return carry
-
-    lax.fori_loop(0, n - 1, rs_step, 0)
-
-    def ag_copy(d, t):
-        chunk = (pos + 1 + n - t) % n if d == 0 else (pos + n - 1 + t) % n
+    sends = [rs_copy(nb) for nb in peers]
+    for c in sends:
+        c.start()
+    acc = x_ref[me].astype(jnp.float32)
+    for nb in peers:
+        pltpu.make_async_remote_copy(
+            src_ref=x_ref.at[nb],
+            dst_ref=rbuf.at[nb],
+            send_sem=rs_send.at[nb],
+            recv_sem=rs_recv.at[nb],
+            device_id=(row, nb),
+            device_id_type=MESH,
+        ).wait_recv()
+        acc = acc + rbuf[nb].astype(jnp.float32)
+    o_ref[me] = acc.astype(o_ref.dtype)
+    for c in sends:
+        c.wait_send()
+
+    def ag_copy(nb):
         return pltpu.make_async_remote_copy(
-            src_ref=o_ref.at[d, chunk],
-            dst_ref=o_ref.at[d, chunk],
-            send_sem=ag_send.at[d, t],
-            recv_sem=ag_recv.at[d, t],
-            device_id=(row, peers[d]),
+            src_ref=o_ref.at[me],
+            dst_ref=o_ref.at[me],
+            send_sem=ag_send.at[nb],
+            recv_sem=ag_recv.at[me],
+            device_id=(row, nb),
             device_id_type=MESH,
         )
 
-    def ag_step(t, carry):
-        copies = [ag_copy(d, t) for d in range(2)]
-        for c in copies:
-            c.start()
-        for c in copies:
-            c.wait_recv()
-        for c in copies:
-            c.wait_send()
-        return carry
-
-    lax.fori_loop(0, n - 1, ag_step, 0)
-
-
-def ring_allreduce(x, n, cid):
-    _, _, rows, cols = x.shape
+    sends = [ag_copy(nb) for nb in peers]
+    for c in sends:
+        c.start()
+    for nb in peers:
+        pltpu.make_async_remote_copy(
+            src_ref=o_ref.at[nb],
+            dst_ref=o_ref.at[nb],
+            send_sem=ag_send.at[nb],
+            recv_sem=ag_recv.at[nb],
+            device_id=(row, nb),
+            device_id_type=MESH,
+        ).wait_recv()
+    for c in sends:
+        c.wait_send()
+
+
+def direct_allreduce(x, n, cid):
+    _, rows, cols = x.shape
     return pl.pallas_call(
-        functools.partial(ring_kernel, n),
+        functools.partial(direct_kernel, n),
         out_shape=jax.ShapeDtypeStruct(x.shape, x.dtype),
         in_specs=[pl.BlockSpec(memory_space=pltpu.VMEM)],
         out_specs=pl.BlockSpec(memory_space=pltpu.VMEM),
         scratch_shapes=[
-            pltpu.VMEM((2, n - 1, rows, cols), x.dtype),
-            pltpu.SemaphoreType.DMA((2, n - 1)),
-            pltpu.SemaphoreType.DMA((2, n - 1)),
-            pltpu.SemaphoreType.DMA((2, n - 1)),
-            pltpu.SemaphoreType.DMA((2, n - 1)),
+            pltpu.VMEM((n, rows, cols), x.dtype),
+            pltpu.SemaphoreType.DMA((n,)),
+            pltpu.SemaphoreType.DMA((n,)),
+            pltpu.SemaphoreType.DMA((n,)),
+            pltpu.SemaphoreType.DMA((n,)),
         ],
         compiler_params=pltpu.CompilerParams(collective_id=cid, has_side_effects=True),
     )(x)
@@ -111,8 +100,8 @@
 def slot_allreduce(slots, n, cid):
     steps, rows, cols = slots.shape
     total = steps * rows
-    chunk = total // (2 * n)
-    out = ring_allreduce(slots.reshape(2, n, chunk, cols), n, cid)
+    chunk = total // n
+    out = direct_allreduce(slots.reshape(n, chunk, cols), n, cid)
     return out.reshape(steps, rows, cols)
 
 

time: 395 us -> 418 us (1.058); the launches traced: 393 us -> 411 us
  Pallas kernels: 283 us -> 301 us
    pallas_call x2, Pallas kernels: 283 us -> 301 us  [direct_allreduce(): pl.pallas_call(functools.partial(direct_kernel, n), out_shape=jax.ShapeDt...]
where the time goes in v2:
time: 418 us; the launch traced here: 411 us
  Pallas kernels  301 us (72%)
  matrix products  41.2 us (10%)
  local copies, waits for them, and re-layouts  35.9 us (9%)
  other arithmetic  24.3 us (6%)
  between operations  9.01 us (2%)
    pallas_call x2, Pallas kernels, direct_allreduce(): pl.pallas_call(functools.partial(direct_kernel, n), out_shape=jax.ShapeDt...  301 us
    dot_general x5, matrix products, pair_terms(): jnp.einsum('hgqk,khd->qhgd', grad_scores, key_heads, preferred_element_ty...  12 us
    another operation x5, other arithmetic, on_device(): summed = slot_allreduce(jnp.stack(terms), n, 1)  11.9 us
    unnamed x71, local copies, waits for them, and re-layouts  10.2 us

profile of v2, /device:TPU:6, one launch (start us, length us, event | category | flops | bytes accessed | tf_op | source)
XLA Modules:
  0.0 410.9 jit_solution(17084046755605013499)
XLA Ops:
  16.2 1.7 reshape.241
  25.2 104.8 %shard_map.103 = bf16[16,64,1024]{2,1,0:T(8,128)(2,1)} custom-call(bf16[16,64,1024]{2,1,0:T(8,128)(2,1)} %broadcast_select_fusion.x_ref), custom_call_target="tpu_custom_call" | custom-call | tf_op jit(solution)/shard_map/pallas_call | solution.py:84
  130.0 1.7 fusion.90
  138.7 1.8 fusion.31
  141.9 2.0 copy.105
  145.6 2.8 fusion.95
  149.7 2.1 maximum_bitcast_fusion
  151.9 1.7 fusion.96
  153.6 1.8 fusion.29
  156.8 2.0 copy.111
  160.5 2.8 fusion.97
  164.6 2.1 maximum_bitcast_fusion.1
  166.7 1.7 fusion.98
  168.5 1.8 fusion.27
  171.9 2.0 copy.117
  175.5 2.7 fusion.99
  179.6 2.1 maximum_bitcast_fusion.2
  181.7 1.7 fusion.100
  183.5 1.8 fusion.25
  186.7 2.0 copy.123
  190.3 2.7 fusion.101
  195.4 4.4 %pad_maximum_fusion = f32[4,256,1024]{2,1,0:T(8,128)} fusion(f32[1,256,1024]{2,1,0:T(8,128)S(1)} %maximum_bitcast_fusion.3, f32[1,256,1024]{2,1,0:T(8,128)} %maximum_bitcast_fusion.2, f32[1,256,1024]{2,1,0:T(8,128)} %maximum_bitcast_fusion.1, f32[1,256,1024]{2,1,0:T(8,128)} %maximum_bitcast_fusion), kind=kLoop, calls=%fused_computation | loop fusion | flops 3145728 | bytes 8388608 | tf_op jit(solution)/shard_map/stack | solution.py:193
  199.8 195.7 %shard_map.104 = f32[16,64,1024]{2,1,0:T(8,128)} custom-call(f32[16,64,1024]{2,1,0:T(8,128)} %bitcast.354), custom_call_target="tpu_custom_call" | custom-call | tf_op jit(solution)/shard_map/pallas_call | solution.py:84
  404.9 6.0 %fusion.63 = (bf16[256,512]{1,0:T(8,128)(2,1)}, bf16[256,512]{1,0:T(8,128)(2,1)}) fusion(f32[4,256,1024]{2,1,0:T(8,128)} %bitcast.353, f32[256,512]{1,0:T(8,128)S(1)} %copy.127, pred[]{:T(512)} %bitcast.97, pred[]{:T(512)} %bitcast.95, pred[]{:T(512)} %bitcast.93, pred[]{:T(512)} %bitcast.53, f32[256,512]{1,0:T(8,128)S(1)} %copy.124), kind=kLoop, calls=%fused_computation.84 | loop fusion | flops 2359296 | bytes 5767172 | tf_op jit(solution)/shard_map/convert_element_type | solution.py:198
  (111 shorter events, 49.8 us)
Async XLA Ops:
  0.6 21.4 %copy-start.5 = (bf16[256,2048]{1,0:T(8,128)(2,1)S(1)}, bf16[256,2048]{1,0:T(8,128)(2,1)}, u32[]{:S(2)}) copy-start(bf16[256,2048]{1,0:T(8,128)(2,1)} %param.11) | copy-start | bytes 3145732
  135.2 3.4 copy-start.6
  136.0 2.6 copy-start.24
  138.6 1.8 copy-start.7
  138.6 1.8 copy-start.19
  138.7 1.8 copy-start.25
  138.7 1.8 copy-start.26
  148.4 5.2 %copy-start.8 = (bf16[256,2048]{0,1:T(8,128)(2,1)S(1)}, bf16[256,2048]{0,1:T(8,128)(2,1)}, u32[]{:S(2)}) copy-start(bf16[256,2048]{0,1:T(8,128)(2,1)} %copy.200) | copy-start | bytes 3145732
  148.4 5.2 %copy-start.22 = (pred[256,256]{0,1:T(8,128)(4,1)S(1)}, pred[256,256]{0,1:T(8,128)(4,1)}, u32[]{:S(2)}) copy-start(pred[256,256]{0,1:T(8,128)(4,1)} %get-tuple-element.25) | copy-start | bytes 196612
  153.6 1.8 copy-start.9
  153.6 1.8 copy-start.18
  153.6 1.8 copy-start.23
  163.2 5.2 %copy-start.10 = (bf16[256,2048]{0,1:T(8,128)(2,1)S(1)}, bf16[256,2048]{0,1:T(8,128)(2,1)}, u32[]{:S(2)}) copy-start(bf16[256,2048]{0,1:T(8,128)(2,1)} %copy.200) | copy-start | bytes 3145732
  163.2 5.2 %copy-start.20 = (pred[256,256]{0,1:T(8,128)(4,1)S(1)}, pred[256,256]{0,1:T(8,128)(4,1)}, u32[]{:S(2)}) copy-start(pred[256,256]{0,1:T(8,128)(4,1)} %get-tuple-element.26) | copy-start | bytes 196612
  168.4 1.8 copy-start.11
  168.4 1.8 copy-start.17
  168.4 1.8 copy-start.21
  168.4 1.8 copy-start.28
  178.3 5.2 %copy-start.12 = (bf16[256,2048]{0,1:T(8,128)(2,1)S(1)}, bf16[256,2048]{0,1:T(8,128)(2,1)}, u32[]{:S(2)}) copy-start(bf16[256,2048]{0,1:T(8,128)(2,1)} %copy.200) | copy-start | bytes 3145732
  183.4 1.8 copy-start.13
  183.4 1.8 copy-start.16
  397.8 2.2 copy-start.1
  397.8 2.8 copy-start.2
  397.8 3.4 copy-start.3
  (7 other events, 10.0 us)

commit v3 on v1

--- a/solution.py
+++ b/solution.py
@@ -26,7 +26,7 @@
     return (1 - q) * (2 * p) + q * (2 * (n - 1 - p) + 1)
 
 
-def ring_kernel(n, x_ref, o_ref, rbuf, rs_send, rs_recv, ag_send, ag_recv):
+def ring_kernel(n, x_ref, o_ref, rbuf, rs_send, rs_recv, ag_send, ag_recv, ready):
     me = lax.axis_index("ctx")
     row = lax.axis_index("dp")
     pos = ring_pos(me, n)
@@ -52,19 +52,33 @@
             device_id_type=MESH,
         )
 
+    first = [rs_copy(d, 0) for d in range(2)]
+    for c in first:
+        c.start()
+
     def rs_step(s, carry):
-        copies = [rs_copy(d, s) for d in range(2)]
-        for c in copies:
-            c.start()
-        for d in range(2):
-            copies[d].wait_recv()
+        for d in range(2):
+            rs_copy(d, s).wait_recv()
             got = (pos + 2 * n - s - 1) % n if d == 0 else (pos + s + 1) % n
             o_ref[d, got] = o_ref[d, got] + rbuf[d, s]
-        for c in copies:
-            c.wait_send()
+
+            @pl.when(s < n - 2)
+            def _():
+                rs_copy(d, s + 1).start()
+
         return carry
 
     lax.fori_loop(0, n - 1, rs_step, 0)
+
+    def rs_drain(s, carry):
+        for d in range(2):
+            rs_copy(d, s).wait_send()
+        return carry
+
+    lax.fori_loop(0, n - 1, rs_drain, 0)
+    for nb in (left, right):
+        pl.semaphore_signal(ready, inc=1, device_id=(row, nb), device_id_type=MESH)
+    pl.semaphore_wait(ready, 2)
 
     def ag_copy(d, t):
         chunk = (pos + 1 + n - t) % n if d == 0 else (pos + n - 1 + t) % n
@@ -77,17 +91,28 @@
             device_id_type=MESH,
         )
 
+    first = [ag_copy(d, 0) for d in range(2)]
+    for c in first:
+        c.start()
+
     def ag_step(t, carry):
-        copies = [ag_copy(d, t) for d in range(2)]
-        for c in copies:
-            c.start()
-        for c in copies:
-            c.wait_recv()
-        for c in copies:
-            c.wait_send()
+        for d in range(2):
+            ag_copy(d, t).wait_recv()
+
+            @pl.when(t < n - 2)
+            def _():
+                ag_copy(d, t + 1).start()
+
         return carry
 
     lax.fori_loop(0, n - 1, ag_step, 0)
+
+    def drain(s, carry):
+        for d in range(2):
+            ag_copy(d, s).wait_send()
+        return carry
+
+    lax.fori_loop(0, n - 1, drain, 0)
 
 
 def ring_allreduce(x, n, cid):
@@ -103,6 +128,7 @@
             pltpu.SemaphoreType.DMA((2, n - 1)),
             pltpu.SemaphoreType.DMA((2, n - 1)),
             pltpu.SemaphoreType.DMA((2, n - 1)),
+            pltpu.SemaphoreType.REGULAR,
         ],
         compiler_params=pltpu.CompilerParams(collective_id=cid, has_side_effects=True),
     )(x)

time: 395 us -> 376 us (0.952)
  Pallas kernels: 283 us -> 262 us
    pallas_call x2, Pallas kernels: 283 us -> 262 us  [ring_allreduce(): pl.pallas_call(functools.partial(ring_kernel, n), out_shape=jax.ShapeDtyp...]
where the time goes in v3:
time: 376 us; the launch traced here: 373 us
  Pallas kernels  262 us (70%)
  matrix products  41.2 us (11%)
  local copies, waits for them, and re-layouts  35.9 us (10%)
  other arithmetic  24.3 us (6%)
  between operations  9.01 us (2%)
    pallas_call x2, Pallas kernels, ring_allreduce(): pl.pallas_call(functools.partial(ring_kernel, n), out_shape=jax.ShapeDtyp...  262 us
    dot_general x5, matrix products, pair_terms(): jnp.einsum('hgqk,khd->qhgd', grad_scores, key_heads, preferred_element_ty...  12 us
    another operation x5, other arithmetic, on_device(): summed = slot_allreduce(jnp.stack(terms), n, 1)  11.9 us
    unnamed x71, local copies, waits for them, and re-layouts  10.1 us
    reshape x5, local copies, waits for them, and re-layouts, pair_terms(): grad_v = jnp.einsum('hgqk,qhgd->khd', probs_low, grad_heads, preferred_el...  8.36 us
    dot_general x5, matrix products, pair_terms(): jnp.einsum('hgqk,qhgd->khd', probs_low, grad_heads, preferred_element_typ...  8.08 us

profile of v3, /device:TPU:6, one launch (start us, length us, event | category | flops | bytes accessed | tf_op | source)
XLA Modules:
  0.0 372.8 jit_solution(16968573008831924375)
XLA Ops:
  16.3 1.7 reshape.244
  25.3 118.5 %shard_map.103 = bf16[2,16,32,1024]{3,2,1,0:T(8,128)(2,1)} custom-call(bf16[2,16,32,1024]{3,2,1,0:T(8,128)(2,1)} %broadcast_select_fusion.x_ref), custom_call_target="tpu_custom_call" | custom-call | tf_op jit(solution)/shard_map/pallas_call | solution.py:120
  143.8 1.7 fusion.90
  152.4 1.8 fusion.31
  155.7 2.0 copy.105
  159.3 2.8 fusion.95
  163.4 2.1 maximum_bitcast_fusion
  165.6 1.7 fusion.96
  167.3 1.8 fusion.29
  170.6 2.0 copy.111
  174.2 2.8 fusion.97
  178.3 2.1 maximum_bitcast_fusion.1
  182.2 1.8 fusion.27
  185.4 2.0 copy.117
  187.5 1.8 fusion.59
  189.2 2.7 fusion.99
  193.3 2.1 maximum_bitcast_fusion.2
  195.4 1.7 fusion.100
  197.2 1.8 fusion.25
  200.4 2.0 copy.123
  204.0 2.7 fusion.101
  209.1 4.4 %pad_maximum_fusion = f32[4,256,1024]{2,1,0:T(8,128)} fusion(f32[1,256,1024]{2,1,0:T(8,128)S(1)} %maximum_bitcast_fusion.3, f32[1,256,1024]{2,1,0:T(8,128)} %maximum_bitcast_fusion.2, f32[1,256,1024]{2,1,0:T(8,128)} %maximum_bitcast_fusion.1, f32[1,256,1024]{2,1,0:T(8,128)} %maximum_bitcast_fusion), kind=kLoop, calls=%fused_computation | loop fusion | flops 3145728 | bytes 8388608 | tf_op jit(solution)/shard_map/stack | solution.py:230
  213.5 143.9 %shard_map.104 = f32[2,16,32,1024]{3,2,1,0:T(8,128)} custom-call(f32[2,16,32,1024]{3,2,1,0:T(8,128)} %bitcast.354), custom_call_target="tpu_custom_call" | custom-call | tf_op jit(solution)/shard_map/pallas_call | solution.py:120
  366.8 6.0 %fusion.63 = (bf16[256,512]{1,0:T(8,128)(2,1)}, bf16[256,512]{1,0:T(8,128)(2,1)}) fusion(f32[4,256,1024]{2,1,0:T(8,128)} %bitcast.353, f32[256,512]{1,0:T(8,128)S(1)} %copy.127, pred[]{:T(512)} %bitcast.97, pred[]{:T(512)} %bitcast.95, pred[]{:T(512)} %bitcast.93, pred[]{:T(512)} %bitcast.53, f32[256,512]{1,0:T(8,128)S(1)} %copy.124), kind=kLoop, calls=%fused_computation.84 | loop fusion | flops 2359296 | bytes 5767172 | tf_op jit(solution)/shard_map/convert_element_type | solution.py:235
  (112 shorter events, 49.8 us)
Async XLA Ops:
  0.6 21.5 %copy-start.5 = (bf16[256,2048]{1,0:T(8,128)(2,1)S(1)}, bf16[256,2048]{1,0:T(8,128)(2,1)}, u32[]{:S(2)}) copy-start(bf16[256,2048]{1,0:T(8,128)(2,1)} %param.11) | copy-start | bytes 3145732
  148.9 3.4 copy-start.6
  149.7 2.6 copy-start.24
  152.4 1.8 copy-start.7
  152.4 1.8 copy-start.19
  152.4 1.8 copy-start.25
  152.4 1.8 copy-start.26
  162.1 5.2 %copy-start.8 = (bf16[256,2048]{0,1:T(8,128)(2,1)S(1)}, bf16[256,2048]{0,1:T(8,128)(2,1)}, u32[]{:S(2)}) copy-start(bf16[256,2048]{0,1:T(8,128)(2,1)} %copy.200) | copy-start | bytes 3145732
  162.1 5.2 %copy-start.22 = (pred[256,256]{0,1:T(8,128)(4,1)S(1)}, pred[256,256]{0,1:T(8,128)(4,1)}, u32[]{:S(2)}) copy-start(pred[256,256]{0,1:T(8,128)(4,1)} %get-tuple-element.25) | copy-start | bytes 196612
  167.3 1.8 copy-start.9
  167.3 1.8 copy-start.18
  167.3 1.8 copy-start.23
  177.0 5.2 %copy-start.10 = (bf16[256,2048]{0,1:T(8,128)(2,1)S(1)}, bf16[256,2048]{0,1:T(8,128)(2,1)}, u32[]{:S(2)}) copy-start(bf16[256,2048]{0,1:T(8,128)(2,1)} %copy.200) | copy-start | bytes 3145732
  177.0 5.2 %copy-start.20 = (pred[256,256]{0,1:T(8,128)(4,1)S(1)}, pred[256,256]{0,1:T(8,128)(4,1)}, u32[]{:S(2)}) copy-start(pred[256,256]{0,1:T(8,128)(4,1)} %get-tuple-element.26) | copy-start | bytes 196612
  182.1 1.8 copy-start.11
  182.2 1.8 copy-start.17
  182.2 1.8 copy-start.21
  182.2 1.8 copy-start.28
  192.0 5.2 %copy-start.12 = (bf16[256,2048]{0,1:T(8,128)(2,1)S(1)}, bf16[256,2048]{0,1:T(8,128)(2,1)}, u32[]{:S(2)}) copy-start(bf16[256,2048]{0,1:T(8,128)(2,1)} %copy.200) | copy-start | bytes 3145732
  197.1 1.8 copy-start.13
  197.2 1.8 copy-start.16
  359.7 2.2 copy-start.1
  359.7 2.8 copy-start.2
  359.7 3.4 copy-start.3
  (7 other events, 10.0 us)

commit v4 on v3

--- a/solution.py
+++ b/solution.py
@@ -26,7 +26,7 @@
     return (1 - q) * (2 * p) + q * (2 * (n - 1 - p) + 1)
 
 
-def ring_kernel(n, x_ref, o_ref, rbuf, rs_send, rs_recv, ag_send, ag_recv, ready):
+def ring_kernel(n, m, x_ref, o_ref, rbuf, rs_send, rs_recv, ag_send, ag_recv, ready):
     me = lax.axis_index("ctx")
     row = lax.axis_index("dp")
     pos = ring_pos(me, n)
@@ -41,38 +41,40 @@
 
     o_ref[...] = x_ref[...]
 
-    def rs_copy(d, s):
+    def rs_copy(d, s, k):
         send = (pos + n - s) % n if d == 0 else (pos + s) % n
         return pltpu.make_async_remote_copy(
-            src_ref=o_ref.at[d, send],
-            dst_ref=rbuf.at[d, s],
-            send_sem=rs_send.at[d, s],
-            recv_sem=rs_recv.at[d, s],
+            src_ref=o_ref.at[d, send, k],
+            dst_ref=rbuf.at[d, s, k],
+            send_sem=rs_send.at[d, s, k],
+            recv_sem=rs_recv.at[d, s, k],
             device_id=(row, peers[d]),
             device_id_type=MESH,
         )
 
-    first = [rs_copy(d, 0) for d in range(2)]
-    for c in first:
-        c.start()
+    for k in range(m):
+        for d in range(2):
+            rs_copy(d, 0, k).start()
 
     def rs_step(s, carry):
-        for d in range(2):
-            rs_copy(d, s).wait_recv()
-            got = (pos + 2 * n - s - 1) % n if d == 0 else (pos + s + 1) % n
-            o_ref[d, got] = o_ref[d, got] + rbuf[d, s]
-
-            @pl.when(s < n - 2)
-            def _():
-                rs_copy(d, s + 1).start()
+        for k in range(m):
+            for d in range(2):
+                rs_copy(d, s, k).wait_recv()
+                got = (pos + 2 * n - s - 1) % n if d == 0 else (pos + s + 1) % n
+                o_ref[d, got, k] = o_ref[d, got, k] + rbuf[d, s, k]
+
+                @pl.when(s < n - 2)
+                def _():
+                    rs_copy(d, s + 1, k).start()
 
         return carry
 
     lax.fori_loop(0, n - 1, rs_step, 0)
 
     def rs_drain(s, carry):
-        for d in range(2):
-            rs_copy(d, s).wait_send()
+        for k in range(m):
+            for d in range(2):
+                rs_copy(d, s, k).wait_send()
         return carry
 
     lax.fori_loop(0, n - 1, rs_drain, 0)
@@ -80,54 +82,56 @@
         pl.semaphore_signal(ready, inc=1, device_id=(row, nb), device_id_type=MESH)
     pl.semaphore_wait(ready, 2)
 
-    def ag_copy(d, t):
+    def ag_copy(d, t, k):
         chunk = (pos + 1 + n - t) % n if d == 0 else (pos + n - 1 + t) % n
         return pltpu.make_async_remote_copy(
-            src_ref=o_ref.at[d, chunk],
-            dst_ref=o_ref.at[d, chunk],
-            send_sem=ag_send.at[d, t],
-            recv_sem=ag_recv.at[d, t],
+            src_ref=o_ref.at[d, chunk, k],
+            dst_ref=o_ref.at[d, chunk, k],
+            send_sem=ag_send.at[d, t, k],
+            recv_sem=ag_recv.at[d, t, k],
             device_id=(row, peers[d]),
             device_id_type=MESH,
         )
 
-    first = [ag_copy(d, 0) for d in range(2)]
-    for c in first:
-        c.start()
+    for k in range(m):
+        for d in range(2):
+            ag_copy(d, 0, k).start()
 
     def ag_step(t, carry):
-        for d in range(2):
-            ag_copy(d, t).wait_recv()
-
-            @pl.when(t < n - 2)
-            def _():
-                ag_copy(d, t + 1).start()
+        for k in range(m):
+            for d in range(2):
+                ag_copy(d, t, k).wait_recv()
+
+                @pl.when(t < n - 2)
+                def _():
+                    ag_copy(d, t + 1, k).start()
 
         return carry
 
     lax.fori_loop(0, n - 1, ag_step, 0)
 
     def drain(s, carry):
-        for d in range(2):
-            ag_copy(d, s).wait_send()
+        for k in range(m):
+            for d in range(2):
+                ag_copy(d, s, k).wait_send()
         return carry
 
     lax.fori_loop(0, n - 1, drain, 0)
 
 
 def ring_allreduce(x, n, cid):
-    _, _, rows, cols = x.shape
+    _, _, m, rows, cols = x.shape
     return pl.pallas_call(
-        functools.partial(ring_kernel, n),
+        functools.partial(ring_kernel, n, m),
         out_shape=jax.ShapeDtypeStruct(x.shape, x.dtype),
         in_specs=[pl.BlockSpec(memory_space=pltpu.VMEM)],
         out_specs=pl.BlockSpec(memory_space=pltpu.VMEM),
         scratch_shapes=[
-            pltpu.VMEM((2, n - 1, rows, cols), x.dtype),
-            pltpu.SemaphoreType.DMA((2, n - 1)),
-            pltpu.SemaphoreType.DMA((2, n - 1)),
-            pltpu.SemaphoreType.DMA((2, n - 1)),
-            pltpu.SemaphoreType.DMA((2, n - 1)),
+            pltpu.VMEM((2, n - 1, m, rows, cols), x.dtype),
+            pltpu.SemaphoreType.DMA((2, n - 1, m)),
+            pltpu.SemaphoreType.DMA((2, n - 1, m)),
+            pltpu.SemaphoreType.DMA((2, n - 1, m)),
+            pltpu.SemaphoreType.DMA((2, n - 1, m)),
             pltpu.SemaphoreType.REGULAR,
         ],
         compiler_params=pltpu.CompilerParams(collective_id=cid, has_side_effects=True),
@@ -137,8 +141,9 @@
 def slot_allreduce(slots, n, cid):
     steps, rows, cols = slots.shape
     total = steps * rows
-    chunk = total // (2 * n)
-    out = ring_allreduce(slots.reshape(2, n, chunk, cols), n, cid)
+    sub = 16 if slots.dtype == jnp.bfloat16 else 8
+    m = total // (2 * n * sub)
+    out = ring_allreduce(slots.reshape(2, n, m, sub, cols), n, cid)
     return out.reshape(steps, rows, cols)
 
 

time: 376 us -> 335 us (0.89)
  Pallas kernels: 262 us -> 223 us
    pallas_call x2, Pallas kernels: 262 us -> 223 us  [ring_allreduce(): pl.pallas_call(functools.partial(ring_kernel, n, m), out_shape=jax.ShapeD...]
where the time goes in v4:
time: 335 us; the launch traced here: 333 us
  Pallas kernels  223 us (67%)
  matrix products  41 us (12%)
  local copies, waits for them, and re-layouts  36.2 us (11%)
  other arithmetic  24.3 us (7%)
  between operations  9.01 us (3%)
    pallas_call x2, Pallas kernels, ring_allreduce(): pl.pallas_call(functools.partial(ring_kernel, n, m), out_shape=jax.ShapeD...  223 us
    dot_general x5, matrix products, pair_terms(): jnp.einsum('hgqk,khd->qhgd', grad_scores, key_heads, preferred_element_ty...  12 us
    another operation x5, other arithmetic, on_device(): summed = slot_allreduce(jnp.stack(terms), n, 1)  11.9 us
    unnamed x71, local copies, waits for them, and re-layouts  10.2 us
    reshape x5, local copies, waits for them, and re-layouts, pair_terms(): grad_v = jnp.einsum('hgqk,qhgd->khd', probs_low, grad_heads, preferred_el...  8.56 us
    dot_general x5, matrix products, pair_terms(): jnp.einsum('hgqk,qhgd->khd', probs_low, grad_heads, preferred_element_typ...  8.08 us
    dot_general x5, matrix products, pair_terms(): jnp.einsum('hgqk,qhgd->khd', grad_scores, query_heads, preferred_element_...  7.24 us
    dot_general x5, matrix products, pair_terms(): jnp.einsum('qhgd,khd->hgqk', grad_heads, value_heads, preferred_element_t...  7.12 us

profile of v4, /device:TPU:6, one launch (start us, length us, event | category | flops | bytes accessed | tf_op | source)
XLA Modules:
  0.0 333.3 jit_solution(17720054384835970385)
XLA Ops:
  16.3 1.7 reshape.244
  25.3 109.0 %shard_map.103 = bf16[2,16,2,16,1024]{4,3,2,1,0:T(8,128)(2,1)} custom-call(bf16[2,16,2,16,1024]{4,3,2,1,0:T(8,128)(2,1)} %broadcast_select_fusion.x_ref), custom_call_target="tpu_custom_call" | custom-call | tf_op jit(solution)/shard_map/pallas_call | solution.py:124
  134.3 1.7 fusion.90
  142.9 1.8 fusion.31
  146.2 2.0 copy.105
  149.8 2.8 fusion.95
  154.0 2.1 maximum_bitcast_fusion
  156.1 1.7 fusion.96
  157.9 1.8 fusion.29
  161.1 2.0 copy.111
  164.7 2.8 fusion.97
  168.8 2.1 maximum_bitcast_fusion.1
  170.9 1.7 fusion.98
  172.7 1.8 fusion.27
  175.9 2.2 copy.117
  179.8 2.7 fusion.99
  183.9 2.1 maximum_bitcast_fusion.2
  186.0 1.7 fusion.100
  187.7 1.8 fusion.25
  191.0 2.0 copy.123
  194.6 2.7 fusion.101
  199.7 4.4 %pad_maximum_fusion = f32[4,256,1024]{2,1,0:T(8,128)} fusion(f32[1,256,1024]{2,1,0:T(8,128)S(1)} %maximum_bitcast_fusion.3, f32[1,256,1024]{2,1,0:T(8,128)} %maximum_bitcast_fusion.2, f32[1,256,1024]{2,1,0:T(8,128)} %maximum_bitcast_fusion.1, f32[1,256,1024]{2,1,0:T(8,128)} %maximum_bitcast_fusion), kind=kLoop, calls=%fused_computation | loop fusion | flops 3145728 | bytes 8388608 | tf_op jit(solution)/shard_map/stack | solution.py:235
  204.1 113.9 %shard_map.104 = f32[2,16,4,8,1024]{4,3,2,1,0:T(8,128)} custom-call(f32[2,16,4,8,1024]{4,3,2,1,0:T(8,128)} %bitcast.354), custom_call_target="tpu_custom_call" | custom-call | tf_op jit(solution)/shard_map/pallas_call | solution.py:124
  327.3 6.0 %fusion.63 = (bf16[256,512]{1,0:T(8,128)(2,1)}, bf16[256,512]{1,0:T(8,128)(2,1)}) fusion(f32[4,256,1024]{2,1,0:T(8,128)} %bitcast.353, f32[256,512]{1,0:T(8,128)S(1)} %copy.127, pred[]{:T(512)} %bitcast.97, pred[]{:T(512)} %bitcast.95, pred[]{:T(512)} %bitcast.93, pred[]{:T(512)} %bitcast.53, f32[256,512]{1,0:T(8,128)S(1)} %copy.124), kind=kLoop, calls=%fused_computation.84 | loop fusion | flops 2359296 | bytes 5767172 | tf_op jit(solution)/shard_map/convert_element_type | solution.py:240
  (112 shorter events, 49.7 us)
Async XLA Ops:
  0.6 21.5 %copy-start.5 = (bf16[256,2048]{1,0:T(8,128)(2,1)S(1)}, bf16[256,2048]{1,0:T(8,128)(2,1)}, u32[]{:S(2)}) copy-start(bf16[256,2048]{1,0:T(8,128)(2,1)} %param.11) | copy-start | bytes 3145732
  139.4 3.5 %copy-start.6 = (bf16[256,2048]{0,1:T(8,128)(2,1)S(1)}, bf16[256,2048]{0,1:T(8,128)(2,1)}, u32[]{:S(2)}) copy-start(bf16[256,2048]{0,1:T(8,128)(2,1)} %copy.200) | copy-start | bytes 3145732
  140.2 2.6 copy-start.24
  142.9 1.8 copy-start.7
  142.9 1.8 copy-start.19
  142.9 1.8 copy-start.25
  142.9 1.8 copy-start.26
  152.6 5.2 %copy-start.8 = (bf16[256,2048]{0,1:T(8,128)(2,1)S(1)}, bf16[256,2048]{0,1:T(8,128)(2,1)}, u32[]{:S(2)}) copy-start(bf16[256,2048]{0,1:T(8,128)(2,1)} %copy.200) | copy-start | bytes 3145732
  152.6 5.2 %copy-start.22 = (pred[256,256]{0,1:T(8,128)(4,1)S(1)}, pred[256,256]{0,1:T(8,128)(4,1)}, u32[]{:S(2)}) copy-start(pred[256,256]{0,1:T(8,128)(4,1)} %get-tuple-element.25) | copy-start | bytes 196612
  157.8 1.8 copy-start.9
  157.8 1.8 copy-start.18
  157.8 1.8 copy-start.23
  167.5 5.2 %copy-start.10 = (bf16[256,2048]{0,1:T(8,128)(2,1)S(1)}, bf16[256,2048]{0,1:T(8,128)(2,1)}, u32[]{:S(2)}) copy-start(bf16[256,2048]{0,1:T(8,128)(2,1)} %copy.200) | copy-start | bytes 3145732
  167.5 5.2 %copy-start.20 = (pred[256,256]{0,1:T(8,128)(4,1)S(1)}, pred[256,256]{0,1:T(8,128)(4,1)}, u32[]{:S(2)}) copy-start(pred[256,256]{0,1:T(8,128)(4,1)} %get-tuple-element.26) | copy-start | bytes 196612
  172.7 1.8 copy-start.11
  172.7 1.8 copy-start.17
  172.7 1.8 copy-start.21
  172.7 1.8 copy-start.28
  182.5 5.2 %copy-start.12 = (bf16[256,2048]{0,1:T(8,128)(2,1)S(1)}, bf16[256,2048]{0,1:T(8,128)(2,1)}, u32[]{:S(2)}) copy-start(bf16[256,2048]{0,1:T(8,128)(2,1)} %copy.200) | copy-start | bytes 3145732
  187.7 1.8 copy-start.13
  187.7 1.8 copy-start.16
  320.2 2.2 copy-start.1
  320.2 2.8 copy-start.2
  320.2 3.4 %copy-start.3 = (f32[4,128,4,256]{3,1,2,0:T(8,128)S(1)}, f32[4,128,4,256]{3,1,2,0:T(8,128)}, u32[]{:S(2)}) copy-start(f32[4,128,4,256]{3,1,2,0:T(8,128)} %fusion.101) | copy-start | bytes 6291460
  (7 other events, 10.0 us)

commit v5 on v4

--- a/solution.py
+++ b/solution.py
@@ -15,34 +15,26 @@
 MESH = pl.DeviceIdType.MESH
 
 
-def ring_pos(c, n):
-    y = c % 2
-    z = c // 2
-    return (1 - y) * z + y * (n - 1 - z)
-
-
-def ring_ctx(p, n):
-    q = p // (n // 2)
-    return (1 - q) * (2 * p) + q * (2 * (n - 1 - p) + 1)
-
-
-def ring_kernel(n, m, x_ref, o_ref, rbuf, rs_send, rs_recv, ag_send, ag_recv, ready):
+def grid_kernel(nz, m, x_ref, o_ref, rbuf, ybuf, rs_send, rs_recv, y_send, y_recv, ag_send,
+                ag_recv, ready):
     me = lax.axis_index("ctx")
     row = lax.axis_index("dp")
-    pos = ring_pos(me, n)
-    right = ring_ctx((pos + 1) % n, n)
-    left = ring_ctx((pos + n - 1) % n, n)
+    z = me // 2
+    y = me % 2
+    right = ((z + 1) % nz) * 2 + y
+    left = ((z + nz - 1) % nz) * 2 + y
+    partner = z * 2 + (1 - y)
     peers = (right, left)
 
     barrier = pltpu.get_barrier_semaphore()
-    for nb in (left, right):
+    for nb in (left, right, partner):
         pl.semaphore_signal(barrier, inc=1, device_id=(row, nb), device_id_type=MESH)
-    pl.semaphore_wait(barrier, 2)
+    pl.semaphore_wait(barrier, 3)
 
     o_ref[...] = x_ref[...]
 
     def rs_copy(d, s, k):
-        send = (pos + n - s) % n if d == 0 else (pos + s) % n
+        send = (z + nz - s) % nz if d == 0 else (z + s) % nz
         return pltpu.make_async_remote_copy(
             src_ref=o_ref.at[d, send, k],
             dst_ref=rbuf.at[d, s, k],
@@ -60,16 +52,38 @@
         for k in range(m):
             for d in range(2):
                 rs_copy(d, s, k).wait_recv()
-                got = (pos + 2 * n - s - 1) % n if d == 0 else (pos + s + 1) % n
+                got = (z + 2 * nz - s - 1) % nz if d == 0 else (z + s + 1) % nz
                 o_ref[d, got, k] = o_ref[d, got, k] + rbuf[d, s, k]
 
-                @pl.when(s < n - 2)
+                @pl.when(s < nz - 2)
                 def _():
                     rs_copy(d, s + 1, k).start()
 
         return carry
 
-    lax.fori_loop(0, n - 1, rs_step, 0)
+    lax.fori_loop(0, nz - 1, rs_step, 0)
+
+    mine = ((z + 1) % nz, (z + nz - 1) % nz)
+
+    def y_copy(d, k):
+        return pltpu.make_async_remote_copy(
+            src_ref=o_ref.at[d, mine[d], k],
+            dst_ref=ybuf.at[d, k],
+            send_sem=y_send.at[d, k],
+            recv_sem=y_recv.at[d, k],
+            device_id=(row, partner),
+            device_id_type=MESH,
+        )
+
+    for k in range(m):
+        for d in range(2):
+            y_copy(d, k).start()
+    for k in range(m):
+        for d in range(2):
+            c = y_copy(d, k)
+            c.wait_recv()
+            c.wait_send()
+            o_ref[d, mine[d], k] = o_ref[d, mine[d], k] + ybuf[d, k]
 
     def rs_drain(s, carry):
         for k in range(m):
@@ -77,13 +91,13 @@
                 rs_copy(d, s, k).wait_send()
         return carry
 
-    lax.fori_loop(0, n - 1, rs_drain, 0)
+    lax.fori_loop(0, nz - 1, rs_drain, 0)
     for nb in (left, right):
         pl.semaphore_signal(ready, inc=1, device_id=(row, nb), device_id_type=MESH)
     pl.semaphore_wait(ready, 2)
 
     def ag_copy(d, t, k):
-        chunk = (pos + 1 + n - t) % n if d == 0 else (pos + n - 1 + t) % n
+        chunk = (z + 1 + nz - t) % nz if d == 0 else (z + nz - 1 + t) % nz
         return pltpu.make_async_remote_copy(
             src_ref=o_ref.at[d, chunk, k],
             dst_ref=o_ref.at[d, chunk, k],
@@ -102,13 +116,13 @@
             for d in range(2):
                 ag_copy(d, t, k).wait_recv()
 
-                @pl.when(t < n - 2)
+                @pl.when(t < nz - 2)
                 def _():
                     ag_copy(d, t + 1, k).start()
 
         return carry
 
-    lax.fori_loop(0, n - 1, ag_step, 0)
+    lax.fori_loop(0, nz - 1, ag_step, 0)
 
     def drain(s, carry):
         for k in range(m):
@@ -116,22 +130,25 @@
                 ag_copy(d, s, k).wait_send()
         return carry
 
-    lax.fori_loop(0, n - 1, drain, 0)
-
-
-def ring_allreduce(x, n, cid):
-    _, _, m, rows, cols = x.shape
+    lax.fori_loop(0, nz - 1, drain, 0)
+
+
+def grid_allreduce(x, cid):
+    _, nz, m, rows, cols = x.shape
     return pl.pallas_call(
-        functools.partial(ring_kernel, n, m),
+        functools.partial(grid_kernel, nz, m),
         out_shape=jax.ShapeDtypeStruct(x.shape, x.dtype),
         in_specs=[pl.BlockSpec(memory_space=pltpu.VMEM)],
         out_specs=pl.BlockSpec(memory_space=pltpu.VMEM),
         scratch_shapes=[
-            pltpu.VMEM((2, n - 1, m, rows, cols), x.dtype),
-            pltpu.SemaphoreType.DMA((2, n - 1, m)),
-            pltpu.SemaphoreType.DMA((2, n - 1, m)),
-            pltpu.SemaphoreType.DMA((2, n - 1, m)),
-            pltpu.SemaphoreType.DMA((2, n - 1, m)),
+            pltpu.VMEM((2, nz - 1, m, rows, cols), x.dtype),
+            pltpu.VMEM((2, m, rows, cols), x.dtype),
+            pltpu.SemaphoreType.DMA((2, nz - 1, m)),
+            pltpu.SemaphoreType.DMA((2, nz - 1, m)),
+            pltpu.SemaphoreType.DMA((2, m)),
+            pltpu.SemaphoreType.DMA((2, m)),
+            pltpu.SemaphoreType.DMA((2, nz - 1, m)),
+            pltpu.SemaphoreType.DMA((2, nz - 1, m)),
             pltpu.SemaphoreType.REGULAR,
         ],
         compiler_params=pltpu.CompilerParams(collective_id=cid, has_side_effects=True),
@@ -142,8 +159,9 @@
     steps, rows, cols = slots.shape
     total = steps * rows
     sub = 16 if slots.dtype == jnp.bfloat16 else 8
-    m = total // (2 * n * sub)
-    out = ring_allreduce(slots.reshape(2, n, m, sub, cols), n, cid)
+    nz = n // 2
+    m = total // (2 * nz * sub)
+    out = grid_allreduce(slots.reshape(2, nz, m, sub, cols), cid)
     return out.reshape(steps, rows, cols)
 
 

time: 335 us -> 266 us (0.79)
  Pallas kernels: 223 us -> 154 us
    pallas_call x2, Pallas kernels: 223 us -> 154 us  [grid_allreduce(): pl.pallas_call(functools.partial(grid_kernel, nz, m), out_shape=jax.Shape...]
where the time goes in v5:
time: 266 us; the launch traced here: 265 us
  Pallas kernels  154 us (58%)
  matrix products  41 us (15%)
  local copies, waits for them, and re-layouts  36.2 us (14%)
  other arithmetic  24.3 us (9%)
  between operations  9.01 us (3%)
    pallas_call x2, Pallas kernels, grid_allreduce(): pl.pallas_call(functools.partial(grid_kernel, nz, m), out_shape=jax.Shape...  154 us
    dot_general x5, matrix products, pair_terms(): jnp.einsum('hgqk,khd->qhgd', grad_scores, key_heads, preferred_element_ty...  12 us
    another operation x5, other arithmetic, on_device(): summed = slot_allreduce(jnp.stack(terms), n, 1)  11.9 us
    unnamed x71, local copies, waits for them, and re-layouts  10.2 us
    reshape x5, local copies, waits for them, and re-layouts, pair_terms(): grad_v = jnp.einsum('hgqk,qhgd->khd', probs_low, grad_heads, preferred_el...  8.56 us
    dot_general x5, matrix products, pair_terms(): jnp.einsum('hgqk,qhgd->khd', probs_low, grad_heads, preferred_element_typ...  8.09 us
    dot_general x5, matrix products, pair_terms(): jnp.einsum('hgqk,qhgd->khd', grad_scores, query_heads, preferred_element_...  7.24 us
    dot_general x5, matrix products, pair_terms(): jnp.einsum('qhgd,khd->hgqk', grad_heads, value_heads, preferred_element_t...  7.12 us

profile of v5, /device:TPU:6, one launch (start us, length us, event | category | flops | bytes accessed | tf_op | source)
XLA Modules:
  0.0 265.0 jit_solution(11186277068590461259)
XLA Ops:
  16.3 1.7 reshape.244
  25.3 69.9 %shard_map.103 = bf16[2,8,4,16,1024]{4,3,2,1,0:T(8,128)(2,1)} custom-call(bf16[2,8,4,16,1024]{4,3,2,1,0:T(8,128)(2,1)} %broadcast_select_fusion.x_ref), custom_call_target="tpu_custom_call" | custom-call | tf_op jit(solution)/shard_map/pallas_call | solution.py:138
  95.2 1.7 fusion.90
  103.8 1.8 fusion.31
  107.1 2.0 copy.105
  110.7 2.8 %fusion.95 = f32[4,128,4,256]{3,1,2,0:T(8,128)} fusion(bf16[256,4,128,1]{0,2,3,1:T(8,128)(2,1)} %bitcast.365, bf16[4,4,256,256]{2,3,1,0:T(8,128)(2,1)S(1)} %fusion.13), kind=kOutput, calls=%fused_computation.140 | convolution fusion | flops 268435456 | bytes 4456448 | tf_op jit(solution)/shard_map/hgqk,khd->qhgd/dot_general | solution.py:190
  114.9 2.1 maximum_bitcast_fusion
  117.0 1.7 fusion.96
  118.8 1.8 fusion.29
  122.0 2.0 copy.111
  125.6 2.8 %fusion.97 = f32[4,128,4,256]{3,1,2,0:T(8,128)} fusion(bf16[256,4,128,1]{0,2,3,1:T(8,128)(2,1)} %bitcast.363, bf16[4,4,256,256]{2,3,1,0:T(8,128)(2,1)S(1)} %fusion.9), kind=kOutput, calls=%fused_computation.142 | convolution fusion | flops 268435456 | bytes 4456448 | tf_op jit(solution)/shard_map/hgqk,khd->qhgd/dot_general | solution.py:190
  129.7 2.1 maximum_bitcast_fusion.1
  131.9 1.7 fusion.98
  133.6 1.8 fusion.27
  136.9 2.2 copy.117
  140.7 2.7 %fusion.99 = f32[4,128,4,256]{3,1,2,0:T(8,128)} fusion(bf16[256,4,128,1]{0,2,3,1:T(8,128)(2,1)} %bitcast.361, bf16[4,4,256,256]{2,3,1,0:T(8,128)(2,1)S(1)} %fusion.5), kind=kOutput, calls=%fused_computation.144 | convolution fusion | flops 268435456 | bytes 4456448 | tf_op jit(solution)/shard_map/hgqk,khd->qhgd/dot_general | solution.py:190
  144.8 2.1 maximum_bitcast_fusion.2
  146.9 1.7 fusion.100
  148.7 1.8 fusion.25
  151.9 2.0 copy.123
  155.5 2.7 %fusion.101 = f32[4,128,4,256]{3,1,2,0:T(8,128)} fusion(bf16[256,4,128,1]{0,2,3,1:T(8,128)(2,1)} %bitcast.359, bf16[4,4,256,256]{2,3,1,0:T(8,128)(2,1)S(1)} %fusion.1), kind=kOutput, calls=%fused_computation.146 | convolution fusion | flops 268435456 | bytes 4456448 | tf_op jit(solution)/shard_map/hgqk,khd->qhgd/dot_general | solution.py:190
  160.6 4.4 %pad_maximum_fusion = f32[4,256,1024]{2,1,0:T(8,128)} fusion(f32[1,256,1024]{2,1,0:T(8,128)S(1)} %maximum_bitcast_fusion.3, f32[1,256,1024]{2,1,0:T(8,128)} %maximum_bitcast_fusion.2, f32[1,256,1024]{2,1,0:T(8,128)} %maximum_bitcast_fusion.1, f32[1,256,1024]{2,1,0:T(8,128)} %maximum_bitcast_fusion), kind=kLoop, calls=%fused_computation | loop fusion | flops 3145728 | bytes 8388608 | tf_op jit(solution)/shard_map/stack | solution.py:253
  165.0 84.6 %shard_map.104 = f32[2,8,8,8,1024]{4,3,2,1,0:T(8,128)} custom-call(f32[2,8,8,8,1024]{4,3,2,1,0:T(8,128)} %bitcast.354), custom_call_target="tpu_custom_call" | custom-call | tf_op jit(solution)/shard_map/pallas_call | solution.py:138
  259.0 6.0 %fusion.63 = (bf16[256,512]{1,0:T(8,128)(2,1)}, bf16[256,512]{1,0:T(8,128)(2,1)}) fusion(f32[4,256,1024]{2,1,0:T(8,128)} %bitcast.353, f32[256,512]{1,0:T(8,128)S(1)} %copy.127, pred[]{:T(512)} %bitcast.97, pred[]{:T(512)} %bitcast.95, pred[]{:T(512)} %bitcast.93, pred[]{:T(512)} %bitcast.53, f32[256,512]{1,0:T(8,128)S(1)} %copy.124), kind=kLoop, calls=%fused_computation.84 | loop fusion | flops 2359296 | bytes 5767172 | tf_op jit(solution)/shard_map/convert_element_type | solution.py:258
  (112 shorter events, 49.7 us)
Async XLA Ops:
  0.6 21.5 %copy-start.5 = (bf16[256,2048]{1,0:T(8,128)(2,1)S(1)}, bf16[256,2048]{1,0:T(8,128)(2,1)}, u32[]{:S(2)}) copy-start(bf16[256,2048]{1,0:T(8,128)(2,1)} %param.11) | copy-start | bytes 3145732
  100.3 3.4 %copy-start.6 = (bf16[256,2048]{0,1:T(8,128)(2,1)S(1)}, bf16[256,2048]{0,1:T(8,128)(2,1)}, u32[]{:S(2)}) copy-start(bf16[256,2048]{0,1:T(8,128)(2,1)} %copy.200) | copy-start | bytes 3145732
  101.2 2.6 copy-start.24
  103.8 1.8 copy-start.7
  103.8 1.8 copy-start.19
  103.8 1.8 copy-start.25
  103.8 1.8 copy-start.26
  113.5 5.2 %copy-start.8 = (bf16[256,2048]{0,1:T(8,128)(2,1)S(1)}, bf16[256,2048]{0,1:T(8,128)(2,1)}, u32[]{:S(2)}) copy-start(bf16[256,2048]{0,1:T(8,128)(2,1)} %copy.200) | copy-start | bytes 3145732
  113.5 5.2 %copy-start.22 = (pred[256,256]{0,1:T(8,128)(4,1)S(1)}, pred[256,256]{0,1:T(8,128)(4,1)}, u32[]{:S(2)}) copy-start(pred[256,256]{0,1:T(8,128)(4,1)} %get-tuple-element.25) | copy-start | bytes 196612
  118.7 1.8 copy-start.9
  118.7 1.8 copy-start.18
  118.8 1.8 copy-start.23
  128.4 5.2 %copy-start.10 = (bf16[256,2048]{0,1:T(8,128)(2,1)S(1)}, bf16[256,2048]{0,1:T(8,128)(2,1)}, u32[]{:S(2)}) copy-start(bf16[256,2048]{0,1:T(8,128)(2,1)} %copy.200) | copy-start | bytes 3145732
  128.4 5.2 %copy-start.20 = (pred[256,256]{0,1:T(8,128)(4,1)S(1)}, pred[256,256]{0,1:T(8,128)(4,1)}, u32[]{:S(2)}) copy-start(pred[256,256]{0,1:T(8,128)(4,1)} %get-tuple-element.26) | copy-start | bytes 196612
  133.6 1.8 copy-start.11
  133.6 1.8 copy-start.17
  133.6 1.8 copy-start.21
  133.6 1.8 copy-start.28
  143.4 5.2 %copy-start.12 = (bf16[256,2048]{0,1:T(8,128)(2,1)S(1)}, bf16[256,2048]{0,1:T(8,128)(2,1)}, u32[]{:S(2)}) copy-start(bf16[256,2048]{0,1:T(8,128)(2,1)} %copy.200) | copy-start | bytes 3145732
  148.6 1.8 copy-start.13
  148.6 1.8 copy-start.16
  251.8 2.2 copy-start.1
  251.8 2.8 %copy-start.2 = (f32[4,128,4,256]{3,1,2,0:T(8,128)S(1)}, f32[4,128,4,256]{3,1,2,0:T(8,128)}, u32[]{:S(2)}) copy-start(f32[4,128,4,256]{3,1,2,0:T(8,128)} %fusion.99) | copy-start | bytes 6291460
  251.8 3.4 %copy-start.3 = (f32[4,128,4,256]{3,1,2,0:T(8,128)S(1)}, f32[4,128,4,256]{3,1,2,0:T(8,128)}, u32[]{:S(2)}) copy-start(f32[4,128,4,256]{3,1,2,0:T(8,128)} %fusion.101) | copy-start | bytes 6291460
  (7 other events, 10.0 us)

commit v6 on v5

--- a/solution.py
+++ b/solution.py
@@ -234,23 +234,34 @@
         kv_slots = jnp.where(is_mine[:, None, None], kv[None], jnp.zeros((), kv.dtype))
         kv_all = slot_allreduce(kv_slots, n, 0)
         local_mask = allowed_rows(block_routes, start, start, tokens, covered, jnp.ones((), jnp.bool_))
-        grad_q, grad_k, grad_v = pair_terms(
-            queries, grad_output, log_norms, grad_dots, key_states, value_states, local_mask
-        )
-        terms = []
+        masks = [local_mask]
         for step in range(steps):
             owner = owner_steps[step]
-            key_part = kv_all[step, :, :features]
-            value_part = kv_all[step, :, features:]
-            step_mask = allowed_rows(
-                block_routes, start, owner * tokens, tokens, jnp.ones((), jnp.bool_), owner != device
+            masks.append(
+                allowed_rows(
+                    block_routes, start, owner * tokens, tokens, jnp.ones((), jnp.bool_), owner != device
+                )
             )
-            term_q, term_k, term_v = pair_terms(
-                queries, grad_output, log_norms, grad_dots, key_part, value_part, step_mask
-            )
-            grad_q = grad_q + term_q
-            terms.append(jnp.concatenate([term_k, term_v], axis=1))
-        summed = slot_allreduce(jnp.stack(terms), n, 1)
+        key_cols = jnp.concatenate(
+            [key_states, kv_all[:, :, :features].reshape(steps * tokens, features)], axis=0
+        )
+        value_cols = jnp.concatenate(
+            [value_states, kv_all[:, :, features:].reshape(steps * tokens, features)], axis=0
+        )
+        grad_q, grad_k_all, grad_v_all = pair_terms(
+            queries, grad_output, log_norms, grad_dots, key_cols, value_cols,
+            jnp.concatenate(masks, axis=1),
+        )
+        grad_k = grad_k_all[:tokens]
+        grad_v = grad_v_all[:tokens]
+        terms = jnp.concatenate(
+            [
+                grad_k_all[tokens:].reshape(steps, tokens, features),
+                grad_v_all[tokens:].reshape(steps, tokens, features),
+            ],
+            axis=2,
+        )
+        summed = slot_allreduce(terms, n, 1)
         for step in range(steps):
             taken = is_mine[step]
             grad_k = grad_k + jnp.where(taken, summed[step, :, :features], jnp.float32(0.0))

time: 266 us -> 257 us (0.966)
  other arithmetic: 24.3 us -> 15.2 us
  matrix products: 41 us -> 44.8 us
  local copies, waits for them, and re-layouts: 36.2 us -> 33.1 us
    another operation x5 -> x0, other arithmetic: 11.9 us -> none  [on_device(): summed = slot_allreduce(jnp.stack(terms), n, 1)]
    reshape x8 -> x0, local copies, waits for them, and re-layouts: 11.5 us -> none  [the longest x5 8.56 us: pair_terms(): grad_v = jnp.einsum('hgqk,qhgd->khd', probs_low, grad_heads, preferred_el...]
    slice x1 -> x10, local copies, waits for them, and re-layouts: 1.73 us -> 12.1 us  [the longest x2 4.52 us: on_device(): grad_k_all[tokens:].reshape(steps, tokens, features)]
    concatenate x0 -> x8, local copies, waits for them, and re-layouts: none -> 9.12 us  [the longest x2 4.95 us: on_device(): jnp.concatenate([grad_k_all[tokens:].reshape(steps, tokens, features), gr...]
    dot_general x5 -> x1, matrix products: 12 us -> 5.74 us  [pair_terms(): jnp.einsum('hgqk,khd->qhgd', grad_scores, key_heads, preferred_element_ty...]
    mul x5 -> x0, local copies, waits for them, and re-layouts: 5.41 us -> none  [pair_terms(): jnp.einsum('hgqk,qhgd->khd', grad_scores, query_heads, preferred_element_...]
    dot_general x5 -> x1, matrix products: 7.12 us -> 12 us  [pair_terms(): jnp.einsum('qhgd,khd->hgqk', grad_heads, value_heads, preferred_element_t...]
    concatenate x0 -> x2, other arithmetic: none -> 4.85 us  [the longest x1 4.71 us: on_device(): jnp.concatenate([grad_k_all[tokens:].reshape(steps, tokens, features), gr...]
where the time goes in v6:
time: 257 us; the launch traced here: 256 us
  Pallas kernels  154 us (60%)
  matrix products  44.8 us (17%)
  local copies, waits for them, and re-layouts  33.1 us (13%)
  other arithmetic  15.2 us (6%)
  between operations  8.72 us (3%)
    pallas_call x2, Pallas kernels, grid_allreduce(): pl.pallas_call(functools.partial(grid_kernel, nz, m), out_shape=jax.Shape...  154 us
    dot_general x1, matrix products, pair_terms(): jnp.einsum('qhgd,khd->hgqk', grad_heads, value_heads, preferred_element_t...  12 us
    dot_general x1, matrix products, pair_terms(): jnp.einsum('qhgd,khd->hgqk', query_heads, key_heads, preferred_element_ty...  10.6 us
    dot_general x1, matrix products, pair_terms(): jnp.einsum('hgqk,qhgd->khd', probs_low, grad_heads, preferred_element_typ...  8.81 us
    dot_general x1, matrix products, pair_terms(): jnp.einsum('hgqk,qhgd->khd', grad_scores, query_heads, preferred_element_...  7.68 us
    convert_element_type x1, other arithmetic, on_device(): grad_v.astype(jnp.bfloat16)  6.27 us
    dot_general x1, matrix products, pair_terms(): jnp.einsum('hgqk,khd->qhgd', grad_scores, key_heads, preferred_element_ty...  5.74 us
    unnamed x23, local copies, waits for them, and re-layouts  5.4 us

profile of v6, /device:TPU:6, one launch (start us, length us, event | category | flops | bytes accessed | tf_op | source)
XLA Modules:
  0.0 256.3 jit_solution(15410385345421549977)
XLA Ops:
  0.7 1.5 copy.53
  3.0 1.4 fusion.36
  7.1 1.4 compare_reduce_fusion
  16.3 1.5 broadcast_select_fusion.x_ref
  17.8 69.7 %shard_map.103 = bf16[2,8,4,16,1024]{4,3,2,1,0:T(8,128)(2,1)} custom-call(bf16[2,8,4,16,1024]{4,3,2,1,0:T(8,128)(2,1)} %broadcast_select_fusion.x_ref), custom_call_target="tpu_custom_call" | custom-call | tf_op jit(solution)/shard_map/pallas_call | solution.py:138
  87.5 2.7 %fusion.34 = (bf16[4,256,512]{2,1,0:T(8,128)(2,1)}, bf16[4,256,512]{2,1,0:T(8,128)(2,1)S(1)}) fusion(bf16[4,256,1024]{2,1,0:T(8,128)(2,1)} %bitcast.119), kind=kLoop, calls=%fused_computation.65 | loop fusion | bytes 4194304 | tf_op jit(solution)/shard_map/slice | solution.py:249
  91.7 10.6 %fusion.3 = f32[4,4,256,1280]{2,3,1,0:T(8,128)} fusion(bf16[256,4,4,128]{0,3,2,1:T(8,128)(2,1)S(1)} %bitcast.120, f32[4,4,256]{2,1,0:T(4,128)S(1)} %sub.42, pred[256,1280]{0,1:T(8,128)(4,1)} %copy-done.8, bf16[1024,4,128]{2,0,1:T(8,128)(2,1)S(1)} %copy.26, bf16[256,4,128]{2,0,1:T(8,128)(2,1)S(1)} %copy.25), kind=kOutput, calls=%fused_computation.5 | convolution fusion | flops 1360527360 | bytes 23674880 | tf_op jit(solution)/shard_map/qhgd,khd->hgqk/dot_general | solution.py:178
  102.3 1.6 copy.54
  105.0 1.4 copy.30
  108.4 12.0 %fusion.1 = bf16[4,4,256,1280]{2,3,1,0:T(8,128)(2,1)} fusion(f32[4,4,256,1280]{2,3,1,0:T(8,128)} %fusion.3, bf16[256,4,4,128]{0,3,2,1:T(8,128)(2,1)S(1)} %bitcast.115, f32[4,4,256]{2,1,0:T(4,128)S(1)} %sub.45, bf16[1024,4,128]{2,0,1:T(8,128)(2,1)S(1)} %copy.30, bf16[256,4,128]{2,0,1:T(8,128)(2,1)S(1)} %copy.29), kind=kOutput, calls=%fused_computation.2 | convolution fusion | flops 1360527360 | bytes 33832960 | tf_op jit(solution)/shard_map/qhgd,khd->hgqk/dot_general | solution.py:184
  120.4 5.7 %multiply_convert_fusion = bf16[4,128,4,256]{3,1,2,0:T(8,128)(2,1)S(1)} fusion(bf16[4,4,256,1280]{2,3,1,0:T(8,128)(2,1)} %fusion.1, bf16[1024,4,128]{2,0,1:T(8,128)(2,1)S(1)} %copy.26, bf16[256,4,128]{2,0,1:T(8,128)(2,1)} %copy-done.3), kind=kOutput, calls=%fused_computation.13 | convolution fusion | flops 1345847296 | bytes 12845056 | tf_op jit(solution)/shard_map/hgqk,khd->qhgd/dot_general | solution.py:190
  126.1 1.4 copy.42
  127.5 8.8 %fusion.6 = f32[1280,4,128]{0,2,1:T(8,128)S(1)} fusion(bf16[256,4,4,128]{0,3,2,1:T(8,128)(2,1)S(1)} %bitcast.116, f32[4,4,256,1280]{2,3,1,0:T(8,128)} %fusion.3), kind=kOutput, calls=%fused_computation.9 | convolution fusion | flops 1347420160 | bytes 24641536 | tf_op jit(solution)/shard_map/hgqk,qhgd->khd/dot_general | solution.py:201
  136.4 1.5 copy-done
  137.9 1.6 slice.102
  139.6 2.0 copy.39
  141.6 1.9 concatenate.39
  143.5 7.7 %fusion.10 = f32[1280,4,128]{0,2,1:T(8,128)S(1)} fusion(bf16[4,4,256,1280]{2,3,1,0:T(8,128)(2,1)} %fusion.1, bf16[256,4,4,128]{0,3,2,1:T(8,128)(2,1)} %bitcast.121), kind=kOutput, calls=%fused_computation.12 | convolution fusion | flops 1342832640 | bytes 14155776 | tf_op jit(solution)/shard_map/hgqk,qhgd->khd/dot_general | solution.py:196
  151.2 1.6 slice.101
  152.8 2.9 %copy.36 = f32[1024,4,128]{2,1,0:T(4,128)} copy(f32[1024,4,128]{0,2,1:T(8,128)} %slice.101) | data formatting | bytes 4194304 | tf_op jit(solution)/shard_map/slice | solution.py:259
  155.7 3.1 %concatenate.38 = f32[2,8,8,8,512]{4,3,2,1,0:T(8,128)} reshape(f32[1024,4,128]{2,1,0:T(4,128)} %copy.36) | data formatting | bytes 4194304 | tf_op jit(solution)/shard_map/concatenate | solution.py:257
  158.7 4.7 %pad_maximum_fusion.x_ref = f32[2,8,8,8,1024]{4,3,2,1,0:T(8,128)} fusion(f32[2,8,8,8,512]{4,3,2,1,0:T(8,128)} %concatenate.39, f32[2,8,8,8,512]{4,3,2,1,0:T(8,128)} %concatenate.38), kind=kLoop, calls=%fused_computation.8 | loop fusion | flops 1048576 | bytes 8388608 | tf_op jit(solution)/shard_map/concatenate | solution.py:257
  163.5 84.6 %shard_map.104 = f32[2,8,8,8,1024]{4,3,2,1,0:T(8,128)} custom-call(f32[2,8,8,8,1024]{4,3,2,1,0:T(8,128)} %pad_maximum_fusion.x_ref), custom_call_target="tpu_custom_call" | custom-call | tf_op jit(solution)/shard_map/pallas_call | solution.py:138
  250.0 6.3 %fusion.15 = (bf16[256,512]{1,0:T(8,128)(2,1)}, bf16[256,512]{1,0:T(8,128)(2,1)}) fusion(f32[4,256,1024]{2,1,0:T(8,128)} %bitcast.114, f32[256,512]{1,0:T(8,128)} %copy.41, pred[]{:T(512)} %bitcast.31, pred[]{:T(512)} %bitcast.29, pred[]{:T(512)} %bitcast.27, pred[]{:T(512)} %bitcast.21, f32[256,512]{1,0:T(8,128)S(1)} %copy.40), kind=kLoop, calls=%fused_computation.22 | loop fusion | flops 2359296 | bytes 5767172 | tf_op jit(solution)/shard_map/convert_element_type | solution.py:269
  (49 shorter events, 9.7 us)
Async XLA Ops:
  0.6 15.0 %copy-start.5 = (bf16[256,512]{1,0:T(8,128)(2,1)S(1)}, bf16[256,512]{1,0:T(8,128)(2,1)}, u32[]{:S(2)}) copy-start(bf16[256,512]{1,0:T(8,128)(2,1)} %param.10) | copy-start | bytes 786436
  0.6 15.0 %copy-start.4 = (bf16[256,512]{1,0:T(8,128)(2,1)S(1)}, bf16[256,512]{1,0:T(8,128)(2,1)}, u32[]{:S(2)}) copy-start(bf16[256,512]{1,0:T(8,128)(2,1)} %param.9) | copy-start | bytes 786436
  2.2 88.8 %copy-start.1 = (bf16[256,2048]{0,1:T(8,128)(2,1)}, bf16[256,2048]{0,1:T(8,128)(2,1)S(1)}, u32[]{:S(2)}) copy-start(bf16[256,2048]{0,1:T(8,128)(2,1)S(1)} %copy.53) | copy-start | bytes 3145732
  2.2 13.8 %copy-start.9 = (s32[4]{0:T(128)S(1)}, s32[4]{0:T(128)}, u32[]{:S(2)}) copy-start(s32[4]{0:T(128)} %param.15) | copy-start | bytes 52
  14.9 0.7 copy-start.8
  91.0 0.7 copy-start.3
  91.7 12.2 %copy-start.7 = (f32[16,256]{1,0:T(8,128)S(1)}, f32[16,256]{1,0:T(8,128)}, u32[]{:S(2)}) copy-start(f32[16,256]{1,0:T(8,128)} %param.13) | copy-start | bytes 49156
  102.3 1.6 copy-start.2
  103.9 2.5 copy-start.6
  136.4 1.6 copy-start
  163.5 84.6 %slice-start = ((f32[1280,4,128]{0,2,1:T(8,128)}), f32[256,4,128]{0,2,1:T(8,128)S(1)}, s32[]{:S(2)}) async-start(f32[1280,4,128]{0,2,1:T(8,128)} %copy-done), calls=%async_computation | async-start | bytes 1048576 | tf_op jit(solution)/shard_map/slice | solution.py:256

commit v7 on v6

--- a/solution.py
+++ b/solution.py
@@ -165,43 +165,67 @@
     return out.reshape(steps, rows, cols)
 
 
+def pair_kernel(scale, group, q_ref, do_ref, k_ref, v_ref, lse_ref, dot_ref, mask_ref, dq_ref,
+                dk_ref, dv_ref):
+    h = pl.program_id(0)
+    qh = q_ref[...]
+    doh = do_ref[...]
+    kg = k_ref[...]
+    vg = v_ref[...]
+    nt = (((1,), (1,)), ((), ()))
+    scores = lax.dot_general(kg, qh, nt, preferred_element_type=jnp.float32) * scale
+    lse = lse_ref[pl.ds(h, 1), :]
+    dots = dot_ref[pl.ds(h, 1), :]
+    probs = jnp.where(mask_ref[...] > 0, jnp.exp(scores - lse), jnp.float32(0.0))
+    grad_probs = lax.dot_general(vg, doh, nt, preferred_element_type=jnp.float32)
+    grad_scores = (probs * (grad_probs - dots)).astype(jnp.bfloat16)
+    probs_low = probs.astype(jnp.bfloat16)
+    tn = (((0,), (0,)), ((), ()))
+    dq = lax.dot_general(grad_scores, kg, tn, preferred_element_type=jnp.float32) * scale
+    dq_ref[...] = dq.astype(dq_ref.dtype)
+    dk = jnp.dot(grad_scores, qh, preferred_element_type=jnp.float32) * scale
+    dv = jnp.dot(probs_low, doh, preferred_element_type=jnp.float32)
+
+    @pl.when(h % group == 0)
+    def _():
+        dk_ref[...] = dk
+        dv_ref[...] = dv
+
+    @pl.when(h % group != 0)
+    def _():
+        dk_ref[...] += dk
+        dv_ref[...] += dv
+
+
 def pair_terms(query_rows, grad_rows, norm_rows, dot_rows, key_rows, value_rows, allowed):
     rows = query_rows.shape[0]
     cols = key_rows.shape[0]
     group = HQ // HK
     scale = 1.0 / math.sqrt(DH)
-    query_heads = query_rows.reshape(rows, HK, group, DH)
-    grad_heads = grad_rows.reshape(rows, HK, group, DH)
-    key_heads = key_rows.reshape(cols, HK, DH)
-    value_heads = value_rows.reshape(cols, HK, DH)
-    scores = (
-        jnp.einsum("qhgd,khd->hgqk", query_heads, key_heads, preferred_element_type=jnp.float32)
-        * scale
-    )
-    norms = norm_rows.reshape(HK, group, rows, 1)
-    dots = dot_rows.reshape(HK, group, rows, 1)
-    probs = jnp.where(allowed, jnp.exp(scores - norms), jnp.float32(0.0))
-    grad_probs = jnp.einsum(
-        "qhgd,khd->hgqk", grad_heads, value_heads, preferred_element_type=jnp.float32
-    )
-    grad_scores = (probs * (grad_probs - dots)).astype(jnp.bfloat16)
-    probs_low = probs.astype(jnp.bfloat16)
-    grad_q = (
-        jnp.einsum(
-            "hgqk,khd->qhgd", grad_scores, key_heads, preferred_element_type=jnp.float32
-        ).reshape(rows, HQ * DH)
-        * scale
-    )
-    grad_k = (
-        jnp.einsum(
-            "hgqk,qhgd->khd", grad_scores, query_heads, preferred_element_type=jnp.float32
-        ).reshape(cols, HK * DH)
-        * scale
-    )
-    grad_v = jnp.einsum(
-        "hgqk,qhgd->khd", probs_low, grad_heads, preferred_element_type=jnp.float32
-    ).reshape(cols, HK * DH)
-    return (grad_q, grad_k, grad_v)
+    return pl.pallas_call(
+        functools.partial(pair_kernel, scale, group),
+        out_shape=(
+            jax.ShapeDtypeStruct((rows, HQ * DH), jnp.bfloat16),
+            jax.ShapeDtypeStruct((cols, HK * DH), jnp.float32),
+            jax.ShapeDtypeStruct((cols, HK * DH), jnp.float32),
+        ),
+        grid=(HQ,),
+        in_specs=[
+            pl.BlockSpec((rows, DH), lambda h: (0, h)),
+            pl.BlockSpec((rows, DH), lambda h: (0, h)),
+            pl.BlockSpec((cols, DH), lambda h: (0, h // group)),
+            pl.BlockSpec((cols, DH), lambda h: (0, h // group)),
+            pl.BlockSpec((HQ, rows), lambda h: (0, 0)),
+            pl.BlockSpec((HQ, rows), lambda h: (0, 0)),
+            pl.BlockSpec((cols, rows), lambda h: (0, 0)),
+        ],
+        out_specs=[
+            pl.BlockSpec((rows, DH), lambda h: (0, h)),
+            pl.BlockSpec((cols, DH), lambda h: (0, h // group)),
+            pl.BlockSpec((cols, DH), lambda h: (0, h // group)),
+        ],
+        compiler_params=pltpu.CompilerParams(dimension_semantics=("arbitrary",)),
+    )(query_rows, grad_rows, key_rows, value_rows, norm_rows, dot_rows, allowed)
 
 
 def allowed_rows(local_routes, query_start, key_start, tokens, widen, active):
@@ -250,7 +274,7 @@
         )
         grad_q, grad_k_all, grad_v_all = pair_terms(
             queries, grad_output, log_norms, grad_dots, key_cols, value_cols,
-            jnp.concatenate(masks, axis=1),
+            jnp.concatenate(masks, axis=1).T.astype(jnp.float32),
         )
         grad_k = grad_k_all[:tokens]
         grad_v = grad_v_all[:tokens]
@@ -266,7 +290,7 @@
             taken = is_mine[step]
             grad_k = grad_k + jnp.where(taken, summed[step, :, :features], jnp.float32(0.0))
             grad_v = grad_v + jnp.where(taken, summed[step, :, features:], jnp.float32(0.0))
-        return (grad_q.astype(jnp.bfloat16), grad_k.astype(jnp.bfloat16), grad_v.astype(jnp.bfloat16))
+        return (grad_q, grad_k.astype(jnp.bfloat16), grad_v.astype(jnp.bfloat16))
 
     return on_device
 

time: 257 us -> 210 us (0.82)
  matrix products: 44.8 us -> 0 us
  local copies, waits for them, and re-layouts: 33.1 us -> 6.14 us
  Pallas kernels: 154 us -> 179 us
    dot_general x5 -> x0, matrix products: 44.8 us -> none  [the longest x1 12 us: pair_terms(): jnp.einsum('qhgd,khd->hgqk', grad_heads, value_heads, preferred_element_t...]
    pallas_call x0 -> x1, Pallas kernels: none -> 24.6 us  [pair_terms(): pl.pallas_call(functools.partial(pair_kernel, scale, group), out_shape=(j...]
    concatenate x8 -> x0, local copies, waits for them, and re-layouts: 9.12 us -> none  [the longest x2 4.95 us: on_device(): jnp.concatenate([grad_k_all[tokens:].reshape(steps, tokens, features), gr...]
    unnamed x23 -> x10, local copies, waits for them, and re-layouts: 5.4 us -> 0.48 us
    slice x2 -> x1, local copies, waits for them, and re-layouts: 4.52 us -> 0.17 us  [on_device(): grad_k_all[tokens:].reshape(steps, tokens, features)]
    reshape x2 -> x0, local copies, waits for them, and re-layouts: 3.1 us -> none  [the longest x1 1.56 us: pair_terms(): grad_heads = grad_rows.reshape(rows, HK, group, DH)]
    convert_element_type x1 -> x2, other arithmetic: 6.27 us -> 7.42 us  [the longest x1 6.23 us: on_device(): return (grad_q, grad_k.astype(jnp.bfloat16), grad_v.astype(jnp.bfloat16))]
where the time goes in v7:
time: 210 us
  Pallas kernels  179 us (85%)
  other arithmetic  16.2 us (8%)
  between operations  8.64 us (4%)
  local copies, waits for them, and re-layouts  6.14 us (3%)
    pallas_call x2, Pallas kernels, grid_allreduce(): pl.pallas_call(functools.partial(grid_kernel, nz, m), out_shape=jax.Shape...  154 us
    pallas_call x1, Pallas kernels, pair_terms(): pl.pallas_call(functools.partial(pair_kernel, scale, group), out_shape=(j...  24.6 us
    convert_element_type x1, other arithmetic, on_device(): return (grad_q, grad_k.astype(jnp.bfloat16), grad_v.astype(jnp.bfloat16))  6.23 us

profile of v7, /device:TPU:6, one launch (start us, length us, event | category | flops | bytes accessed | tf_op | source)
XLA Modules:
  0.0 209.8 jit_solution(4858053433782333646)
XLA Ops:
  0.6 1.1 pad_maximum_fusion.3
  1.7 0.3 broadcast_in_dim.42
  2.0 0.1 broadcast_in_dim.38
  2.2 0.1 broadcast_in_dim.40
  2.3 1.6 broadcast_select_fusion.x_ref
  3.8 69.7 %shard_map.103 = bf16[2,8,4,16,1024]{4,3,2,1,0:T(8,128)(2,1)} custom-call(bf16[2,8,4,16,1024]{4,3,2,1,0:T(8,128)(2,1)} %broadcast_select_fusion.x_ref), custom_call_target="tpu_custom_call" | custom-call | tf_op jit(solution)/shard_map/pallas_call | solution.py:138
  73.6 1.7 fusion.18
  75.3 1.7 pad_maximum_fusion.1
  77.0 0.7 fusion.20
  80.5 0.7 compare_reduce_fusion
  81.2 0.7 and_dynamic-update-slice_fusion.4
  83.2 0.1 and_dynamic-update-slice_fusion.3
  84.7 0.1 and_dynamic-update-slice_fusion.2
  86.1 0.1 and_dynamic-update-slice_fusion.1
  87.5 0.1 and_dynamic-update-slice_fusion
  87.6 1.2 convert_bitcast_fusion.mask_ref
  88.8 24.6 %shard_map.104 = (bf16[256,2048]{1,0:T(8,128)(2,1)}, f32[1280,512]{1,0:T(8,128)}, f32[1280,512]{1,0:T(8,128)}) custom-call(bf16[256,2048]{1,0:T(8,128)(2,1)} %q_ref.1, bf16[256,2048]{1,0:T(8,128)(2,1)} %do_ref.1, bf16[1280,512]{1,0:T(8,128)(2,1)} %get-tuple-element.28.k_ref, bf16[1280,512]{1,0:T(8,128)(2,1)} %get-tuple-element.29.v_ref, f32[16,256]{1,0:T(8,128)} %lse_ref.1, ...), custom_call_target="tpu_custom_call" | custom-call | tf_op jit(solution)/shard_map/pallas_call | solution.py:205
  113.4 1.9 slice.75
  115.3 0.5 copy-done
  115.7 0.2 slice.74
  115.9 2.4 %pad_maximum_fusion.x_ref = f32[2,8,8,8,1024]{4,3,2,1,0:T(8,128)} fusion(f32[2,8,8,8,512]{4,3,2,1,0:T(8,128)S(1)} %bitcast.68, f32[2,8,8,8,512]{4,3,2,1,0:T(8,128)S(1)} %bitcast.69), kind=kLoop, calls=%fused_computation | loop fusion | flops 1048576 | bytes 8388608 | tf_op jit(solution)/shard_map/concatenate | solution.py:281
  118.3 84.6 %shard_map.105 = f32[2,8,8,8,1024]{4,3,2,1,0:T(8,128)} custom-call(f32[2,8,8,8,1024]{4,3,2,1,0:T(8,128)} %pad_maximum_fusion.x_ref), custom_call_target="tpu_custom_call" | custom-call | tf_op jit(solution)/shard_map/pallas_call | solution.py:138
  202.9 0.7 fusion.19
  203.5 6.2 %fusion.2 = (bf16[256,512]{1,0:T(8,128)(2,1)}, bf16[256,512]{1,0:T(8,128)(2,1)}) fusion(f32[4,256,1024]{2,1,0:T(8,128)} %bitcast.65, f32[1280,512]{1,0:T(8,128)} %get-tuple-element.8, pred[]{:T(512)} %bitcast.18, pred[]{:T(512)} %bitcast.16, pred[]{:T(512)} %bitcast.14, pred[]{:T(512)} %bitcast.9, f32[1280,512]{1,0:T(8,128)S(1)} %copy-done), kind=kLoop, calls=%fused_computation.8 | loop fusion | flops 2359296 | bytes 5767172 | tf_op jit(solution)/shard_map/convert_element_type | solution.py:293
  (15 shorter events, 0.1 us)
Async XLA Ops:
  0.6 1.4 copy-start.3
  73.5 1.8 copy-start.1
  73.6 1.8 copy-start.2
  75.3 5.1 %copy-start.4 = (s32[1,4]{1,0:T(1,128)S(1)}, s32[1,4]{1,0:T(1,128)}, u32[]{:S(2)}) copy-start(s32[1,4]{1,0:T(1,128)} %param.14) | copy-start | bytes 52
  113.4 2.4 %copy-start = (f32[1280,512]{1,0:T(8,128)S(1)}, f32[1280,512]{1,0:T(8,128)}, u32[]{:S(2)}) copy-start(f32[1280,512]{1,0:T(8,128)} %get-tuple-element.7) | copy-start | bytes 7864324

commit v8 on v7

--- a/solution.py
+++ b/solution.py
@@ -165,67 +165,86 @@
     return out.reshape(steps, rows, cols)
 
 
-def pair_kernel(scale, group, q_ref, do_ref, k_ref, v_ref, lse_ref, dot_ref, mask_ref, dq_ref,
-                dk_ref, dv_ref):
+def pair_kernel(scale, group, slabs, flag_ref, q_ref, do_ref, k_ref, v_ref, lse_ref, dot_ref,
+                dq_ref, dk_ref, dv_ref, dq_acc):
     h = pl.program_id(0)
     qh = q_ref[...]
     doh = do_ref[...]
-    kg = k_ref[...]
-    vg = v_ref[...]
-    nt = (((1,), (1,)), ((), ()))
-    scores = lax.dot_general(kg, qh, nt, preferred_element_type=jnp.float32) * scale
     lse = lse_ref[pl.ds(h, 1), :]
     dots = dot_ref[pl.ds(h, 1), :]
-    probs = jnp.where(mask_ref[...] > 0, jnp.exp(scores - lse), jnp.float32(0.0))
-    grad_probs = lax.dot_general(vg, doh, nt, preferred_element_type=jnp.float32)
-    grad_scores = (probs * (grad_probs - dots)).astype(jnp.bfloat16)
-    probs_low = probs.astype(jnp.bfloat16)
+    nt = (((1,), (1,)), ((), ()))
     tn = (((0,), (0,)), ((), ()))
-    dq = lax.dot_general(grad_scores, kg, tn, preferred_element_type=jnp.float32) * scale
-    dq_ref[...] = dq.astype(dq_ref.dtype)
-    dk = jnp.dot(grad_scores, qh, preferred_element_type=jnp.float32) * scale
-    dv = jnp.dot(probs_low, doh, preferred_element_type=jnp.float32)
-
-    @pl.when(h % group == 0)
-    def _():
-        dk_ref[...] = dk
-        dv_ref[...] = dv
-
-    @pl.when(h % group != 0)
-    def _():
-        dk_ref[...] += dk
-        dv_ref[...] += dv
-
-
-def pair_terms(query_rows, grad_rows, norm_rows, dot_rows, key_rows, value_rows, allowed):
+    cols = BLK
+    dq_acc[...] = jnp.zeros_like(dq_acc)
+    for j in range(slabs):
+        active = flag_ref[j] > 0
+
+        @pl.when(active)
+        def _():
+            kj = k_ref[j * cols:(j + 1) * cols, :]
+            vj = v_ref[j * cols:(j + 1) * cols, :]
+            scores = lax.dot_general(kj, qh, nt, preferred_element_type=jnp.float32) * scale
+            probs = jnp.exp(scores - lse)
+            if j == 0:
+                key_pos = lax.broadcasted_iota(jnp.int32, probs.shape, 0)
+                query_pos = lax.broadcasted_iota(jnp.int32, probs.shape, 1)
+                probs = jnp.where(key_pos <= query_pos, probs, jnp.float32(0.0))
+            grad_probs = lax.dot_general(vj, doh, nt, preferred_element_type=jnp.float32)
+            grad_scores = (probs * (grad_probs - dots)).astype(jnp.bfloat16)
+            probs_low = probs.astype(jnp.bfloat16)
+            dq_acc[...] += lax.dot_general(grad_scores, kj, tn, preferred_element_type=jnp.float32)
+            dk = jnp.dot(grad_scores, qh, preferred_element_type=jnp.float32) * scale
+            dv = jnp.dot(probs_low, doh, preferred_element_type=jnp.float32)
+
+            @pl.when(h % group == 0)
+            def _():
+                dk_ref[j] = dk
+                dv_ref[j] = dv
+
+            @pl.when(h % group != 0)
+            def _():
+                dk_ref[j] += dk
+                dv_ref[j] += dv
+
+        @pl.when(jnp.logical_not(active) & (h % group == 0))
+        def _():
+            dk_ref[j] = jnp.zeros(dk_ref.shape[1:], dk_ref.dtype)
+            dv_ref[j] = jnp.zeros(dv_ref.shape[1:], dv_ref.dtype)
+
+    dq_ref[...] = (dq_acc[...] * scale).astype(dq_ref.dtype)
+
+
+def pair_terms(flags, query_rows, grad_rows, norm_rows, dot_rows, key_rows, value_rows):
     rows = query_rows.shape[0]
     cols = key_rows.shape[0]
+    slabs = cols // BLK
     group = HQ // HK
     scale = 1.0 / math.sqrt(DH)
     return pl.pallas_call(
-        functools.partial(pair_kernel, scale, group),
+        functools.partial(pair_kernel, scale, group, slabs),
         out_shape=(
             jax.ShapeDtypeStruct((rows, HQ * DH), jnp.bfloat16),
-            jax.ShapeDtypeStruct((cols, HK * DH), jnp.float32),
-            jax.ShapeDtypeStruct((cols, HK * DH), jnp.float32),
+            jax.ShapeDtypeStruct((slabs, BLK, HK * DH), jnp.float32),
+            jax.ShapeDtypeStruct((slabs, BLK, HK * DH), jnp.float32),
         ),
         grid=(HQ,),
         in_specs=[
+            pl.BlockSpec(memory_space=pltpu.SMEM),
             pl.BlockSpec((rows, DH), lambda h: (0, h)),
             pl.BlockSpec((rows, DH), lambda h: (0, h)),
             pl.BlockSpec((cols, DH), lambda h: (0, h // group)),
             pl.BlockSpec((cols, DH), lambda h: (0, h // group)),
             pl.BlockSpec((HQ, rows), lambda h: (0, 0)),
             pl.BlockSpec((HQ, rows), lambda h: (0, 0)),
-            pl.BlockSpec((cols, rows), lambda h: (0, 0)),
         ],
         out_specs=[
             pl.BlockSpec((rows, DH), lambda h: (0, h)),
-            pl.BlockSpec((cols, DH), lambda h: (0, h // group)),
-            pl.BlockSpec((cols, DH), lambda h: (0, h // group)),
+            pl.BlockSpec((slabs, BLK, DH), lambda h: (0, 0, h // group)),
+            pl.BlockSpec((slabs, BLK, DH), lambda h: (0, 0, h // group)),
         ],
+        scratch_shapes=[pltpu.VMEM((rows, DH), jnp.float32)],
         compiler_params=pltpu.CompilerParams(dimension_semantics=("arbitrary",)),
-    )(query_rows, grad_rows, key_rows, value_rows, norm_rows, dot_rows, allowed)
+    )(flags, query_rows, grad_rows, key_rows, value_rows, norm_rows, dot_rows)
 
 
 def allowed_rows(local_routes, query_start, key_start, tokens, widen, active):
@@ -257,39 +276,24 @@
         kv = jnp.concatenate([key_states, value_states], axis=1)
         kv_slots = jnp.where(is_mine[:, None, None], kv[None], jnp.zeros((), kv.dtype))
         kv_all = slot_allreduce(kv_slots, n, 0)
-        local_mask = allowed_rows(block_routes, start, start, tokens, covered, jnp.ones((), jnp.bool_))
-        masks = [local_mask]
-        for step in range(steps):
-            owner = owner_steps[step]
-            masks.append(
-                allowed_rows(
-                    block_routes, start, owner * tokens, tokens, jnp.ones((), jnp.bool_), owner != device
-                )
-            )
+        listed = jnp.any(block_routes[0][None, :] == owner_steps[:, None], axis=1)
+        remote = listed & (owner_steps != device) & (owner_steps < device)
+        flags = jnp.concatenate([jnp.ones((1,), jnp.int32), remote.astype(jnp.int32)])
         key_cols = jnp.concatenate(
             [key_states, kv_all[:, :, :features].reshape(steps * tokens, features)], axis=0
         )
         value_cols = jnp.concatenate(
             [value_states, kv_all[:, :, features:].reshape(steps * tokens, features)], axis=0
         )
-        grad_q, grad_k_all, grad_v_all = pair_terms(
-            queries, grad_output, log_norms, grad_dots, key_cols, value_cols,
-            jnp.concatenate(masks, axis=1).T.astype(jnp.float32),
-        )
-        grad_k = grad_k_all[:tokens]
-        grad_v = grad_v_all[:tokens]
-        terms = jnp.concatenate(
-            [
-                grad_k_all[tokens:].reshape(steps, tokens, features),
-                grad_v_all[tokens:].reshape(steps, tokens, features),
-            ],
-            axis=2,
-        )
+        grad_q, dk_slabs, dv_slabs = pair_terms(
+            flags, queries, grad_output, log_norms, grad_dots, key_cols, value_cols
+        )
+        terms = jnp.concatenate([dk_slabs[1:], dv_slabs[1:]], axis=2)
         summed = slot_allreduce(terms, n, 1)
-        for step in range(steps):
-            taken = is_mine[step]
-            grad_k = grad_k + jnp.where(taken, summed[step, :, :features], jnp.float32(0.0))
-            grad_v = grad_v + jnp.where(taken, summed[step, :, features:], jnp.float32(0.0))
+        held = lax.dynamic_index_in_dim(summed, jnp.argmax(is_mine), keepdims=False)
+        held = jnp.where(covered, held, jnp.float32(0.0))
+        grad_k = dk_slabs[0] + held[:, :features]
+        grad_v = dv_slabs[0] + held[:, features:]
         return (grad_q, grad_k.astype(jnp.bfloat16), grad_v.astype(jnp.bfloat16))
 
     return on_device

time: 210 us -> 217 us (1.033)
  Pallas kernels: 179 us -> 195 us
  between operations: 8.64 us -> 2.8 us
    pallas_call x2, Pallas kernels: 154 us -> 179 us  [grid_allreduce(): pl.pallas_call(functools.partial(grid_kernel, nz, m), out_shape=jax.Shape...]
    pallas_call x1, Pallas kernels: 24.6 us -> 16 us  [pair_terms(): pl.pallas_call(functools.partial(pair_kernel, scale, group, slabs), out_s...]
    convert_element_type x1, other arithmetic: 6.23 us -> 1.98 us  [on_device(): return (grad_q, grad_k.astype(jnp.bfloat16), grad_v.astype(jnp.bfloat16))]
where the time goes in v8:
time: 217 us
  Pallas kernels  195 us (90%)
  other arithmetic  14.1 us (6%)
  local copies, waits for them, and re-layouts  4.83 us (2%)
  between operations  2.8 us (1%)
    pallas_call x2, Pallas kernels, grid_allreduce(): pl.pallas_call(functools.partial(grid_kernel, nz, m), out_shape=jax.Shape...  179 us
    pallas_call x1, Pallas kernels, pair_terms(): pl.pallas_call(functools.partial(pair_kernel, scale, group, slabs), out_s...  16 us

profile of v8, /device:TPU:6, one launch (start us, length us, event | category | flops | bytes accessed | tf_op | source)
XLA Modules:
  0.0 216.5 jit_solution(15060898080681232758)
XLA Ops:
  0.6 0.9 compare_reduce_fusion
  1.5 1.3 fusion.2
  2.8 0.6 add_convert_fusion.flag_ref
  3.4 0.1 broadcast_in_dim.35
  3.5 0.1 broadcast_in_dim.36
  3.5 0.1 broadcast_in_dim.37
  3.6 0.7 iota_reduce_fusion
  6.4 1.1 pad_maximum_fusion.3
  7.5 0.3 broadcast_in_dim.39
  7.8 1.6 broadcast_select_fusion.x_ref
  9.3 69.7 %shard_map.103 = bf16[2,8,4,16,1024]{4,3,2,1,0:T(8,128)(2,1)} custom-call(bf16[2,8,4,16,1024]{4,3,2,1,0:T(8,128)(2,1)} %broadcast_select_fusion.x_ref), custom_call_target="tpu_custom_call" | custom-call | tf_op jit(solution)/shard_map/pallas_call | solution.py:138
  79.1 0.0 copy-start.1
  79.1 0.0 copy-start.2
  79.1 1.7 fusion.3
  80.8 0.0 copy-done.1
  80.8 1.7 pad_maximum_fusion.1
  82.5 16.0 %shard_map.104 = (bf16[256,2048]{1,0:T(8,128)(2,1)}, f32[5,256,512]{2,1,0:T(8,128)}, f32[5,256,512]{2,1,0:T(8,128)}) custom-call(s32[5]{0:T(128)} %add_convert_fusion.flag_ref, bf16[256,2048]{1,0:T(8,128)(2,1)} %q_ref.1, bf16[256,2048]{1,0:T(8,128)(2,1)} %do_ref.1, bf16[1280,512]{1,0:T(8,128)(2,1)} %get-tuple-element.18.k_ref, ...), custom_call_target="tpu_custom_call" | custom-call | tf_op jit(solution)/shard_map/pallas_call | solution.py:223
  98.6 1.9 slice.27
  100.5 0.4 copy-done
  100.9 0.2 slice.28
  101.2 2.3 %pad_maximum_fusion = f32[4,256,1024]{2,1,0:T(8,128)} fusion(f32[4,256,512]{2,1,0:T(8,128)S(1)} %slice.28, f32[4,256,512]{2,1,0:T(8,128)S(1)} %slice.27), kind=kLoop, calls=%fused_computation | loop fusion | flops 1048576 | bytes 8388608 | tf_op jit(solution)/shard_map/concatenate | solution.py:291
  103.5 109.1 %shard_map.105 = f32[2,8,8,8,1024]{4,3,2,1,0:T(8,128)} custom-call(f32[2,8,8,8,1024]{4,3,2,1,0:T(8,128)} %bitcast.13), custom_call_target="tpu_custom_call" | custom-call | tf_op jit(solution)/shard_map/pallas_call | solution.py:138
  212.6 1.9 select_bitcast_fusion
  214.5 2.0 fusion
  (2 shorter events, 0.0 us)
Async XLA Ops:
  79.1 1.8 copy-start.1
  79.1 1.8 copy-start.2
  98.6 2.4 %copy-start = (f32[5,256,512]{2,1,0:T(8,128)S(1)}, f32[5,256,512]{2,1,0:T(8,128)}, u32[]{:S(2)}) copy-start(f32[5,256,512]{2,1,0:T(8,128)} %get-tuple-element.9) | copy-start | bytes 7864324

commit v9 on v7

--- a/solution.py
+++ b/solution.py
@@ -165,9 +165,20 @@
     return out.reshape(steps, rows, cols)
 
 
-def pair_kernel(scale, group, q_ref, do_ref, k_ref, v_ref, lse_ref, dot_ref, mask_ref, dq_ref,
-                dk_ref, dv_ref):
+def pair_kernel(scale, group, flag_ref, q_ref, do_ref, k_ref, v_ref, lse_ref, dot_ref, dq_ref,
+                dk_ref, dv_ref, mask_ref):
     h = pl.program_id(0)
+
+    @pl.when(h == 0)
+    def _():
+        key_pos = lax.broadcasted_iota(jnp.int32, (BLK, BLK), 0)
+        query_pos = lax.broadcasted_iota(jnp.int32, (BLK, BLK), 1)
+        mask_ref[0:BLK, :] = jnp.where(key_pos <= query_pos, jnp.float32(1.0), jnp.float32(0.0))
+        for j in range(1, mask_ref.shape[0] // BLK):
+            mask_ref[j * BLK:(j + 1) * BLK, :] = jnp.full(
+                (BLK, mask_ref.shape[1]), flag_ref[j].astype(jnp.float32), jnp.float32
+            )
+
     qh = q_ref[...]
     doh = do_ref[...]
     kg = k_ref[...]
@@ -197,7 +208,7 @@
         dv_ref[...] += dv
 
 
-def pair_terms(query_rows, grad_rows, norm_rows, dot_rows, key_rows, value_rows, allowed):
+def pair_terms(flags, query_rows, grad_rows, norm_rows, dot_rows, key_rows, value_rows):
     rows = query_rows.shape[0]
     cols = key_rows.shape[0]
     group = HQ // HK
@@ -211,21 +222,22 @@
         ),
         grid=(HQ,),
         in_specs=[
+            pl.BlockSpec(memory_space=pltpu.SMEM),
             pl.BlockSpec((rows, DH), lambda h: (0, h)),
             pl.BlockSpec((rows, DH), lambda h: (0, h)),
             pl.BlockSpec((cols, DH), lambda h: (0, h // group)),
             pl.BlockSpec((cols, DH), lambda h: (0, h // group)),
             pl.BlockSpec((HQ, rows), lambda h: (0, 0)),
             pl.BlockSpec((HQ, rows), lambda h: (0, 0)),
-            pl.BlockSpec((cols, rows), lambda h: (0, 0)),
         ],
         out_specs=[
             pl.BlockSpec((rows, DH), lambda h: (0, h)),
             pl.BlockSpec((cols, DH), lambda h: (0, h // group)),
             pl.BlockSpec((cols, DH), lambda h: (0, h // group)),
         ],
+        scratch_shapes=[pltpu.VMEM((cols, rows), jnp.float32)],
         compiler_params=pltpu.CompilerParams(dimension_semantics=("arbitrary",)),
-    )(query_rows, grad_rows, key_rows, value_rows, norm_rows, dot_rows, allowed)
+    )(flags, query_rows, grad_rows, key_rows, value_rows, norm_rows, dot_rows)
 
 
 def allowed_rows(local_routes, query_start, key_start, tokens, widen, active):
@@ -257,15 +269,9 @@
         kv = jnp.concatenate([key_states, value_states], axis=1)
         kv_slots = jnp.where(is_mine[:, None, None], kv[None], jnp.zeros((), kv.dtype))
         kv_all = slot_allreduce(kv_slots, n, 0)
-        local_mask = allowed_rows(block_routes, start, start, tokens, covered, jnp.ones((), jnp.bool_))
-        masks = [local_mask]
-        for step in range(steps):
-            owner = owner_steps[step]
-            masks.append(
-                allowed_rows(
-                    block_routes, start, owner * tokens, tokens, jnp.ones((), jnp.bool_), owner != device
-                )
-            )
+        listed = jnp.any(block_routes[0][None, :] == owner_steps[:, None], axis=1)
+        remote = listed & (owner_steps != device) & (owner_steps < device)
+        flags = jnp.concatenate([jnp.ones((1,), jnp.int32), remote.astype(jnp.int32)])
         key_cols = jnp.concatenate(
             [key_states, kv_all[:, :, :features].reshape(steps * tokens, features)], axis=0
         )
@@ -273,11 +279,8 @@
             [value_states, kv_all[:, :, features:].reshape(steps * tokens, features)], axis=0
         )
         grad_q, grad_k_all, grad_v_all = pair_terms(
-            queries, grad_output, log_norms, grad_dots, key_cols, value_cols,
-            jnp.concatenate(masks, axis=1).T.astype(jnp.float32),
-        )
-        grad_k = grad_k_all[:tokens]
-        grad_v = grad_v_all[:tokens]
+            flags, queries, grad_output, log_norms, grad_dots, key_cols, value_cols
+        )
         terms = jnp.concatenate(
             [
                 grad_k_all[tokens:].reshape(steps, tokens, features),
@@ -286,10 +289,10 @@
             axis=2,
         )
         summed = slot_allreduce(terms, n, 1)
-        for step in range(steps):
-            taken = is_mine[step]
-            grad_k = grad_k + jnp.where(taken, summed[step, :, :features], jnp.float32(0.0))
-            grad_v = grad_v + jnp.where(taken, summed[step, :, features:], jnp.float32(0.0))
+        held = lax.dynamic_index_in_dim(summed, jnp.argmax(is_mine), keepdims=False)
+        held = jnp.where(covered, held, jnp.float32(0.0))
+        grad_k = grad_k_all[:tokens] + held[:, :features]
+        grad_v = grad_v_all[:tokens] + held[:, features:]
         return (grad_q, grad_k.astype(jnp.bfloat16), grad_v.astype(jnp.bfloat16))
 
     return on_device

time: 210 us -> 202 us (0.962)
  between operations: 8.64 us -> 2.8 us
    convert_element_type x1, other arithmetic: 6.23 us -> 1.98 us  [on_device(): return (grad_q, grad_k.astype(jnp.bfloat16), grad_v.astype(jnp.bfloat16))]
where the time goes in v9:
time: 202 us; the launch traced here: 201 us
  Pallas kernels  180 us (89%)
  other arithmetic  14.1 us (7%)
  local copies, waits for them, and re-layouts  4.79 us (2%)
  between operations  2.8 us (1%)
    pallas_call x2, Pallas kernels, grid_allreduce(): pl.pallas_call(functools.partial(grid_kernel, nz, m), out_shape=jax.Shape...  154 us
    pallas_call x1, Pallas kernels, pair_terms(): pl.pallas_call(functools.partial(pair_kernel, scale, group), out_shape=(j...  25.2 us

profile of v9, /device:TPU:6, one launch (start us, length us, event | category | flops | bytes accessed | tf_op | source)
XLA Modules:
  0.0 201.2 jit_solution(5122369084464161448)
XLA Ops:
  0.6 0.9 compare_reduce_fusion
  1.5 1.3 fusion.2
  2.8 0.6 add_convert_fusion.flag_ref
  3.4 0.1 broadcast_in_dim.35
  3.5 0.1 broadcast_in_dim.36
  3.5 0.1 broadcast_in_dim.37
  3.6 0.7 iota_reduce_fusion
  6.4 1.1 pad_maximum_fusion.3
  7.5 0.3 broadcast_in_dim.39
  7.8 1.6 broadcast_select_fusion.x_ref
  9.3 69.7 %shard_map.103 = bf16[2,8,4,16,1024]{4,3,2,1,0:T(8,128)(2,1)} custom-call(bf16[2,8,4,16,1024]{4,3,2,1,0:T(8,128)(2,1)} %broadcast_select_fusion.x_ref), custom_call_target="tpu_custom_call" | custom-call | tf_op jit(solution)/shard_map/pallas_call | solution.py:138
  79.1 0.0 copy-start.1
  79.1 0.0 copy-start.2
  79.1 1.7 fusion.3
  80.8 0.0 copy-done.1
  80.8 1.7 pad_maximum_fusion.1
  82.5 25.2 %shard_map.104 = (bf16[256,2048]{1,0:T(8,128)(2,1)}, f32[1280,512]{1,0:T(8,128)}, f32[1280,512]{1,0:T(8,128)}) custom-call(s32[5]{0:T(128)} %add_convert_fusion.flag_ref, bf16[256,2048]{1,0:T(8,128)(2,1)} %q_ref.1, bf16[256,2048]{1,0:T(8,128)(2,1)} %do_ref.1, bf16[1280,512]{1,0:T(8,128)(2,1)} %get-tuple-element.18.k_ref, ...), custom_call_target="tpu_custom_call" | custom-call | tf_op jit(solution)/shard_map/pallas_call | solution.py:216
  107.8 1.9 slice.27
  109.7 0.4 copy-done
  110.1 0.2 slice.28
  110.3 2.3 %pad_maximum_fusion.x_ref = f32[2,8,8,8,1024]{4,3,2,1,0:T(8,128)} fusion(f32[2,8,8,8,512]{4,3,2,1,0:T(8,128)S(1)} %bitcast.13, f32[2,8,8,8,512]{4,3,2,1,0:T(8,128)S(1)} %bitcast.12), kind=kLoop, calls=%fused_computation | loop fusion | flops 1048576 | bytes 8388608 | tf_op jit(solution)/shard_map/concatenate | solution.py:284
  112.7 84.6 %shard_map.105 = f32[2,8,8,8,1024]{4,3,2,1,0:T(8,128)} custom-call(f32[2,8,8,8,1024]{4,3,2,1,0:T(8,128)} %pad_maximum_fusion.x_ref), custom_call_target="tpu_custom_call" | custom-call | tf_op jit(solution)/shard_map/pallas_call | solution.py:138
  197.3 1.9 select_bitcast_fusion
  199.2 2.0 fusion
  (2 shorter events, 0.0 us)
Async XLA Ops:
  79.1 1.8 copy-start.1
  79.1 1.8 copy-start.2
  107.8 2.4 %copy-start = (f32[1280,512]{1,0:T(8,128)S(1)}, f32[1280,512]{1,0:T(8,128)}, u32[]{:S(2)}) copy-start(f32[1280,512]{1,0:T(8,128)} %get-tuple-element.9) | copy-start | bytes 7864324

commit v10 on v9

--- a/solution.py
+++ b/solution.py
@@ -165,9 +165,12 @@
     return out.reshape(steps, rows, cols)
 
 
-def pair_kernel(scale, group, flag_ref, q_ref, do_ref, k_ref, v_ref, lse_ref, dot_ref, dq_ref,
-                dk_ref, dv_ref, mask_ref):
+def pair_kernel(scale, group, flag_ref, q_ref, do_ref, k_ref, v_ref, kv_ref, lse_ref, dot_ref,
+                dq_ref, dk_ref, dv_ref, terms_ref, mask_ref):
     h = pl.program_id(0)
+    g = h // group
+    steps, tokens, width = kv_ref.shape
+    features = width // 2
 
     @pl.when(h == 0)
     def _():
@@ -179,10 +182,12 @@
                 (BLK, mask_ref.shape[1]), flag_ref[j].astype(jnp.float32), jnp.float32
             )
 
+    k_lane = pl.ds(pl.multiple_of(g * DH, DH), DH)
+    v_lane = pl.ds(pl.multiple_of(features + g * DH, DH), DH)
     qh = q_ref[...]
     doh = do_ref[...]
-    kg = k_ref[...]
-    vg = v_ref[...]
+    kg = jnp.concatenate([k_ref[...], kv_ref[:, :, k_lane].reshape(steps * tokens, DH)], axis=0)
+    vg = jnp.concatenate([v_ref[...], kv_ref[:, :, v_lane].reshape(steps * tokens, DH)], axis=0)
     nt = (((1,), (1,)), ((), ()))
     scores = lax.dot_general(kg, qh, nt, preferred_element_type=jnp.float32) * scale
     lse = lse_ref[pl.ds(h, 1), :]
@@ -196,48 +201,59 @@
     dq_ref[...] = dq.astype(dq_ref.dtype)
     dk = jnp.dot(grad_scores, qh, preferred_element_type=jnp.float32) * scale
     dv = jnp.dot(probs_low, doh, preferred_element_type=jnp.float32)
+    dk_far = dk[tokens:].reshape(steps, tokens, DH)
+    dv_far = dv[tokens:].reshape(steps, tokens, DH)
 
     @pl.when(h % group == 0)
     def _():
-        dk_ref[...] = dk
-        dv_ref[...] = dv
+        dk_ref[...] = dk[:tokens]
+        dv_ref[...] = dv[:tokens]
+        terms_ref[:, :, k_lane] = dk_far
+        terms_ref[:, :, v_lane] = dv_far
 
     @pl.when(h % group != 0)
     def _():
-        dk_ref[...] += dk
-        dv_ref[...] += dv
-
-
-def pair_terms(flags, query_rows, grad_rows, norm_rows, dot_rows, key_rows, value_rows):
+        dk_ref[...] += dk[:tokens]
+        dv_ref[...] += dv[:tokens]
+        terms_ref[:, :, k_lane] += dk_far
+        terms_ref[:, :, v_lane] += dv_far
+
+
+def pair_terms(flags, query_rows, grad_rows, norm_rows, dot_rows, key_rows, value_rows, kv_all):
     rows = query_rows.shape[0]
-    cols = key_rows.shape[0]
+    tokens = key_rows.shape[0]
+    steps, _, width = kv_all.shape
+    cols = tokens * (1 + steps)
     group = HQ // HK
     scale = 1.0 / math.sqrt(DH)
     return pl.pallas_call(
         functools.partial(pair_kernel, scale, group),
         out_shape=(
             jax.ShapeDtypeStruct((rows, HQ * DH), jnp.bfloat16),
-            jax.ShapeDtypeStruct((cols, HK * DH), jnp.float32),
-            jax.ShapeDtypeStruct((cols, HK * DH), jnp.float32),
+            jax.ShapeDtypeStruct((tokens, HK * DH), jnp.float32),
+            jax.ShapeDtypeStruct((tokens, HK * DH), jnp.float32),
+            jax.ShapeDtypeStruct((steps, tokens, width), jnp.float32),
         ),
         grid=(HQ,),
         in_specs=[
             pl.BlockSpec(memory_space=pltpu.SMEM),
             pl.BlockSpec((rows, DH), lambda h: (0, h)),
             pl.BlockSpec((rows, DH), lambda h: (0, h)),
-            pl.BlockSpec((cols, DH), lambda h: (0, h // group)),
-            pl.BlockSpec((cols, DH), lambda h: (0, h // group)),
+            pl.BlockSpec((tokens, DH), lambda h: (0, h // group)),
+            pl.BlockSpec((tokens, DH), lambda h: (0, h // group)),
+            pl.BlockSpec((steps, tokens, width), lambda h: (0, 0, 0)),
             pl.BlockSpec((HQ, rows), lambda h: (0, 0)),
             pl.BlockSpec((HQ, rows), lambda h: (0, 0)),
         ],
         out_specs=[
             pl.BlockSpec((rows, DH), lambda h: (0, h)),
-            pl.BlockSpec((cols, DH), lambda h: (0, h // group)),
-            pl.BlockSpec((cols, DH), lambda h: (0, h // group)),
+            pl.BlockSpec((tokens, DH), lambda h: (0, h // group)),
+            pl.BlockSpec((tokens, DH), lambda h: (0, h // group)),
+            pl.BlockSpec((steps, tokens, width), lambda h: (0, 0, 0)),
         ],
         scratch_shapes=[pltpu.VMEM((cols, rows), jnp.float32)],
         compiler_params=pltpu.CompilerParams(dimension_semantics=("arbitrary",)),
-    )(flags, query_rows, grad_rows, key_rows, value_rows, norm_rows, dot_rows)
+    )(flags, query_rows, grad_rows, key_rows, value_rows, kv_all, norm_rows, dot_rows)
 
 
 def allowed_rows(local_routes, query_start, key_start, tokens, widen, active):
@@ -272,27 +288,14 @@
         listed = jnp.any(block_routes[0][None, :] == owner_steps[:, None], axis=1)
         remote = listed & (owner_steps != device) & (owner_steps < device)
         flags = jnp.concatenate([jnp.ones((1,), jnp.int32), remote.astype(jnp.int32)])
-        key_cols = jnp.concatenate(
-            [key_states, kv_all[:, :, :features].reshape(steps * tokens, features)], axis=0
-        )
-        value_cols = jnp.concatenate(
-            [value_states, kv_all[:, :, features:].reshape(steps * tokens, features)], axis=0
-        )
-        grad_q, grad_k_all, grad_v_all = pair_terms(
-            flags, queries, grad_output, log_norms, grad_dots, key_cols, value_cols
-        )
-        terms = jnp.concatenate(
-            [
-                grad_k_all[tokens:].reshape(steps, tokens, features),
-                grad_v_all[tokens:].reshape(steps, tokens, features),
-            ],
-            axis=2,
+        grad_q, grad_k, grad_v, terms = pair_terms(
+            flags, queries, grad_output, log_norms, grad_dots, key_states, value_states, kv_all
         )
         summed = slot_allreduce(terms, n, 1)
         held = lax.dynamic_index_in_dim(summed, jnp.argmax(is_mine), keepdims=False)
         held = jnp.where(covered, held, jnp.float32(0.0))
-        grad_k = grad_k_all[:tokens] + held[:, :features]
-        grad_v = grad_v_all[:tokens] + held[:, features:]
+        grad_k = grad_k + held[:, :features]
+        grad_v = grad_v + held[:, features:]
         return (grad_q, grad_k.astype(jnp.bfloat16), grad_v.astype(jnp.bfloat16))
 
     return on_device

time: 202 us -> 197 us (0.975)
  other arithmetic: 14.1 us -> 9.09 us
  local copies, waits for them, and re-layouts: 4.79 us -> 0.51 us
  Pallas kernels: 180 us -> 184 us
    pallas_call x1, Pallas kernels: 25.2 us -> 29.6 us  [pair_terms(): pl.pallas_call(functools.partial(pair_kernel, scale, group), out_shape=(j...]
    concatenate x2 -> x0, other arithmetic: 4.04 us -> none  [the longest x1 2.34 us: on_device(): jnp.concatenate([grad_k_all[tokens:].reshape(steps, tokens, features), gr...]
    slice x3 -> x0, local copies, waits for them, and re-layouts: 3.82 us -> none  [the longest x1 1.91 us: on_device(): grad_k_all[tokens:].reshape(steps, tokens, features)]
where the time goes in v10:
time: 197 us; the launch traced here: 196 us
  Pallas kernels  184 us (93%)
  other arithmetic  9.09 us (5%)
  between operations  2.78 us (1%)
    pallas_call x2, Pallas kernels, grid_allreduce(): pl.pallas_call(functools.partial(grid_kernel, nz, m), out_shape=jax.Shape...  154 us
    pallas_call x1, Pallas kernels, pair_terms(): pl.pallas_call(functools.partial(pair_kernel, scale, group), out_shape=(j...  29.6 us

profile of v10, /device:TPU:6, one launch (start us, length us, event | category | flops | bytes accessed | tf_op | source)
XLA Modules:
  0.0 196.5 jit_solution(8678358086261426457)
XLA Ops:
  0.6 0.9 compare_reduce_fusion
  1.5 1.3 fusion.2
  2.8 0.6 add_convert_fusion.flag_ref
  3.4 0.1 broadcast_in_dim.35
  3.5 0.1 broadcast_in_dim.36
  3.5 0.1 broadcast_in_dim.37
  3.6 0.7 iota_reduce_fusion
  6.4 1.1 pad_maximum_fusion
  7.5 0.3 broadcast_in_dim.39
  7.8 1.6 broadcast_select_fusion.x_ref
  9.3 69.7 %shard_map.103 = bf16[2,8,4,16,1024]{4,3,2,1,0:T(8,128)(2,1)} custom-call(bf16[2,8,4,16,1024]{4,3,2,1,0:T(8,128)(2,1)} %broadcast_select_fusion.x_ref), custom_call_target="tpu_custom_call" | custom-call | tf_op jit(solution)/shard_map/pallas_call | solution.py:138
  79.1 29.6 %shard_map.104 = (bf16[256,2048]{1,0:T(8,128)(2,1)}, f32[256,512]{1,0:T(8,128)}, f32[256,512]{1,0:T(8,128)}, f32[4,256,1024]{2,1,0:T(8,128)}) custom-call(s32[5]{0:T(128)} %add_convert_fusion.flag_ref, bf16[256,2048]{1,0:T(8,128)(2,1)} %q_ref.1, bf16[256,2048]{1,0:T(8,128)(2,1)} %do_ref.1, bf16[256,512]{1,0:T(8,128)(2,1)} %k_ref.1, bf16[256,512]{1,0:T(8,128)(2,1)} %v_ref.1, ...), custom_call_target="tpu_custom_call" | custom-call | tf_op jit(solution)/shard_map/pallas_call | solution.py:229
  108.7 84.7 %shard_map.105 = f32[2,8,8,8,1024]{4,3,2,1,0:T(8,128)} custom-call(f32[2,8,8,8,1024]{4,3,2,1,0:T(8,128)} %bitcast.10), custom_call_target="tpu_custom_call" | custom-call | tf_op jit(solution)/shard_map/pallas_call | solution.py:138
  193.4 0.0 copy-start
  193.5 0.0 copy-start.1
  193.5 2.0 %select_bitcast_fusion = f32[256,1024]{1,0:T(8,128)S(1)} fusion(f32[4,256,1024]{2,1,0:T(8,128)} %bitcast.9, s32[]{:T(128)S(6)} %select_n.26, pred[]{:T(512)} %get-tuple-element.13), kind=kLoop, calls=%fused_computation.1 | loop fusion | flops 262144 | bytes 2097157 | tf_op jit(solution)/shard_map/jit(_where)/select_n | solution.py:296
  195.5 0.0 copy-done
  195.5 0.0 copy-done.1
  195.5 0.9 fusion
Async XLA Ops:
  193.4 2.1 %copy-start = (f32[256,512]{1,0:T(8,128)S(1)}, f32[256,512]{1,0:T(8,128)}, u32[]{:S(2)}) copy-start(f32[256,512]{1,0:T(8,128)} %get-tuple-element.9) | copy-start | bytes 1572868
  193.5 2.1 %copy-start.1 = (f32[256,512]{1,0:T(8,128)S(1)}, f32[256,512]{1,0:T(8,128)}, u32[]{:S(2)}) copy-start(f32[256,512]{1,0:T(8,128)} %get-tuple-element.12) | copy-start | bytes 1572868

commit v11 on v10

--- a/solution.py
+++ b/solution.py
@@ -15,8 +15,9 @@
 MESH = pl.DeviceIdType.MESH
 
 
-def grid_kernel(nz, m, x_ref, o_ref, rbuf, ybuf, rs_send, rs_recv, y_send, y_recv, ag_send,
-                ag_recv, ready):
+def grid_kernel(nz, m, n_in, *refs):
+    ins = refs[:n_in]
+    o_ref, rbuf, ybuf, rs_send, rs_recv, y_send, y_recv, ag_send, ag_recv, ready = refs[n_in:]
     me = lax.axis_index("ctx")
     row = lax.axis_index("dp")
     z = me // 2
@@ -31,7 +32,14 @@
         pl.semaphore_signal(barrier, inc=1, device_id=(row, nb), device_id_type=MESH)
     pl.semaphore_wait(barrier, 3)
 
-    o_ref[...] = x_ref[...]
+    if n_in == 1:
+        o_ref[...] = ins[0][...]
+    else:
+        flag_ref, kv_ref = ins
+        per = kv_ref.shape[0]
+        for i in range(flag_ref.shape[0]):
+            d, c = divmod(i * per, nz)
+            o_ref[d, c:c + per] = jnp.where(flag_ref[i] > 0, kv_ref[...], jnp.zeros((), kv_ref.dtype))
 
     def rs_copy(d, s, k):
         send = (z + nz - s) % nz if d == 0 else (z + s) % nz
@@ -133,12 +141,17 @@
     lax.fori_loop(0, nz - 1, drain, 0)
 
 
-def grid_allreduce(x, cid):
-    _, nz, m, rows, cols = x.shape
+def grid_allreduce(x, cid, shape=None, flags=None):
+    shape = x.shape if shape is None else shape
+    _, nz, m, rows, cols = shape
+    ins = (x,) if flags is None else (flags, x)
+    specs = [pl.BlockSpec(memory_space=pltpu.VMEM)]
+    if flags is not None:
+        specs = [pl.BlockSpec(memory_space=pltpu.SMEM)] + specs
     return pl.pallas_call(
-        functools.partial(grid_kernel, nz, m),
-        out_shape=jax.ShapeDtypeStruct(x.shape, x.dtype),
-        in_specs=[pl.BlockSpec(memory_space=pltpu.VMEM)],
+        functools.partial(grid_kernel, nz, m, len(ins)),
+        out_shape=jax.ShapeDtypeStruct(shape, x.dtype),
+        in_specs=specs,
         out_specs=pl.BlockSpec(memory_space=pltpu.VMEM),
         scratch_shapes=[
             pltpu.VMEM((2, nz - 1, m, rows, cols), x.dtype),
@@ -152,7 +165,7 @@
             pltpu.SemaphoreType.REGULAR,
         ],
         compiler_params=pltpu.CompilerParams(collective_id=cid, has_side_effects=True),
-    )(x)
+    )(*ins)
 
 
 def slot_allreduce(slots, n, cid):
@@ -283,8 +296,14 @@
         is_mine = owner_steps == device
         covered = jnp.any(is_mine)
         kv = jnp.concatenate([key_states, value_states], axis=1)
-        kv_slots = jnp.where(is_mine[:, None, None], kv[None], jnp.zeros((), kv.dtype))
-        kv_all = slot_allreduce(kv_slots, n, 0)
+        nz = n // 2
+        sub = 16
+        m = steps * tokens // (2 * nz * sub)
+        per = 2 * nz // steps
+        kv_all = grid_allreduce(
+            kv.reshape(per, m, sub, 2 * features), 0,
+            shape=(2, nz, m, sub, 2 * features), flags=is_mine.astype(jnp.int32),
+        ).reshape(steps, tokens, 2 * features)
         listed = jnp.any(block_routes[0][None, :] == owner_steps[:, None], axis=1)
         remote = listed & (owner_steps != device) & (owner_steps < device)
         flags = jnp.concatenate([jnp.ones((1,), jnp.int32), remote.astype(jnp.int32)])

time: 197 us -> 196 us (level)
  no operation moved by 1% of the time
where the time goes in v11:
time: 196 us
  Pallas kernels  183 us (93%)
  other arithmetic  9.4 us (5%)
  between operations  2.77 us (1%)
    pallas_call x2, Pallas kernels, grid_allreduce(): pl.pallas_call(functools.partial(grid_kernel, nz, m, len(ins)), out_shape...  154 us
    pallas_call x1, Pallas kernels, pair_terms(): pl.pallas_call(functools.partial(pair_kernel, scale, group), out_shape=(j...  29.6 us

profile of v11, /device:TPU:6, one launch (start us, length us, event | category | flops | bytes accessed | tf_op | source)
XLA Modules:
  0.0 195.6 jit_solution(18152221497887711589)
XLA Ops:
  0.6 0.9 compare_reduce_fusion
  1.5 1.8 fusion.2
  3.3 0.6 add_convert_fusion.flag_ref
  3.9 1.4 iota_reduce_fusion
  7.3 1.9 pad_maximum_fusion
  9.2 69.2 %shard_map.103 = bf16[2,8,4,16,1024]{4,3,2,1,0:T(8,128)(2,1)} custom-call(s32[4]{0:T(128)} %get-tuple-element.16.refs_0_, bf16[4,4,16,1024]{3,2,1,0:T(8,128)(2,1)} %bitcast.10), custom_call_target="tpu_custom_call" | custom-call | tf_op jit(solution)/shard_map/pallas_call | solution.py:151
  78.5 29.6 %shard_map.104 = (bf16[256,2048]{1,0:T(8,128)(2,1)}, f32[256,512]{1,0:T(8,128)}, f32[256,512]{1,0:T(8,128)}, f32[4,256,1024]{2,1,0:T(8,128)}) custom-call(s32[5]{0:T(128)} %add_convert_fusion.flag_ref, bf16[256,2048]{1,0:T(8,128)(2,1)} %q_ref.1, bf16[256,2048]{1,0:T(8,128)(2,1)} %do_ref.1, bf16[256,512]{1,0:T(8,128)(2,1)} %k_ref.1, bf16[256,512]{1,0:T(8,128)(2,1)} %v_ref.1, ...), custom_call_target="tpu_custom_call" | custom-call | tf_op jit(solution)/shard_map/pallas_call | solution.py:242
  108.1 0.0 copy-start
  108.1 0.0 copy-start.1
  108.1 84.6 %shard_map.105 = f32[2,8,8,8,1024]{4,3,2,1,0:T(8,128)} custom-call(f32[2,8,8,8,1024]{4,3,2,1,0:T(8,128)} %bitcast.9), custom_call_target="tpu_custom_call" | custom-call | tf_op jit(solution)/shard_map/pallas_call | solution.py:151
  192.7 1.9 select_bitcast_fusion
  194.7 0.0 copy-done
  194.7 0.0 copy-done.1
  194.7 0.9 fusion
Async XLA Ops:
  108.1 86.6 %copy-start = (f32[256,512]{1,0:T(8,128)S(1)}, f32[256,512]{1,0:T(8,128)}, u32[]{:S(2)}) copy-start(f32[256,512]{1,0:T(8,128)} %get-tuple-element.9) | copy-start | bytes 1572868
  108.1 86.6 %copy-start.1 = (f32[256,512]{1,0:T(8,128)S(1)}, f32[256,512]{1,0:T(8,128)}, u32[]{:S(2)}) copy-start(f32[256,512]{1,0:T(8,128)} %get-tuple-element.12) | copy-start | bytes 1572868

commit v12 on v11

--- a/solution.py
+++ b/solution.py
@@ -171,7 +171,7 @@
 def slot_allreduce(slots, n, cid):
     steps, rows, cols = slots.shape
     total = steps * rows
-    sub = 16 if slots.dtype == jnp.bfloat16 else 8
+    sub = 16
     nz = n // 2
     m = total // (2 * nz * sub)
     out = grid_allreduce(slots.reshape(2, nz, m, sub, cols), cid)

time: 196 us -> 195 us (level)
  no operation moved by 1% of the time
where the time goes in v12:
time: 195 us
  Pallas kernels  183 us (94%)
  other arithmetic  9.4 us (5%)
  between operations  2.77 us (1%)
    pallas_call x2, Pallas kernels, grid_allreduce(): pl.pallas_call(functools.partial(grid_kernel, nz, m, len(ins)), out_shape...  153 us
    pallas_call x1, Pallas kernels, pair_terms(): pl.pallas_call(functools.partial(pair_kernel, scale, group), out_shape=(j...  29.6 us

profile of v12, /device:TPU:6, one launch (start us, length us, event | category | flops | bytes accessed | tf_op | source)
XLA Modules:
  0.0 194.9 jit_solution(7281144627482474303)
XLA Ops:
  0.6 0.9 compare_reduce_fusion
  1.5 1.8 fusion.2
  3.3 0.6 add_convert_fusion.flag_ref
  3.9 1.4 iota_reduce_fusion
  7.3 1.9 pad_maximum_fusion
  9.2 69.2 %shard_map.103 = bf16[2,8,4,16,1024]{4,3,2,1,0:T(8,128)(2,1)} custom-call(s32[4]{0:T(128)} %get-tuple-element.16.refs_0_, bf16[4,4,16,1024]{3,2,1,0:T(8,128)(2,1)} %bitcast.10), custom_call_target="tpu_custom_call" | custom-call | tf_op jit(solution)/shard_map/pallas_call | solution.py:151
  78.5 29.6 %shard_map.104 = (bf16[256,2048]{1,0:T(8,128)(2,1)}, f32[256,512]{1,0:T(8,128)}, f32[256,512]{1,0:T(8,128)}, f32[4,256,1024]{2,1,0:T(8,128)}) custom-call(s32[5]{0:T(128)} %add_convert_fusion.flag_ref, bf16[256,2048]{1,0:T(8,128)(2,1)} %q_ref.1, bf16[256,2048]{1,0:T(8,128)(2,1)} %do_ref.1, bf16[256,512]{1,0:T(8,128)(2,1)} %k_ref.1, bf16[256,512]{1,0:T(8,128)(2,1)} %v_ref.1, ...), custom_call_target="tpu_custom_call" | custom-call | tf_op jit(solution)/shard_map/pallas_call | solution.py:242
  108.1 0.0 copy-start
  108.1 0.0 copy-start.1
  108.1 83.9 %shard_map.105 = f32[2,8,4,16,1024]{4,3,2,1,0:T(8,128)} custom-call(f32[2,8,4,16,1024]{4,3,2,1,0:T(8,128)} %bitcast.9), custom_call_target="tpu_custom_call" | custom-call | tf_op jit(solution)/shard_map/pallas_call | solution.py:151
  192.0 1.9 select_bitcast_fusion
  194.0 0.0 copy-done
  194.0 0.0 copy-done.1
  194.0 0.9 fusion
Async XLA Ops:
  108.1 85.9 %copy-start = (f32[256,512]{1,0:T(8,128)S(1)}, f32[256,512]{1,0:T(8,128)}, u32[]{:S(2)}) copy-start(f32[256,512]{1,0:T(8,128)} %get-tuple-element.9) | copy-start | bytes 1572868
  108.1 85.9 %copy-start.1 = (f32[256,512]{1,0:T(8,128)S(1)}, f32[256,512]{1,0:T(8,128)}, u32[]{:S(2)}) copy-start(f32[256,512]{1,0:T(8,128)} %get-tuple-element.12) | copy-start | bytes 1572868

commit v13 on v11

--- a/solution.py
+++ b/solution.py
@@ -35,11 +35,14 @@
     if n_in == 1:
         o_ref[...] = ins[0][...]
     else:
-        flag_ref, kv_ref = ins
-        per = kv_ref.shape[0]
+        flag_ref, k_ref, v_ref = ins
+        per = k_ref.shape[0]
+        half = k_ref.shape[-1]
+        zero = jnp.zeros((), k_ref.dtype)
         for i in range(flag_ref.shape[0]):
             d, c = divmod(i * per, nz)
-            o_ref[d, c:c + per] = jnp.where(flag_ref[i] > 0, kv_ref[...], jnp.zeros((), kv_ref.dtype))
+            o_ref[d, c:c + per, :, :, :half] = jnp.where(flag_ref[i] > 0, k_ref[...], zero)
+            o_ref[d, c:c + per, :, :, half:] = jnp.where(flag_ref[i] > 0, v_ref[...], zero)
 
     def rs_copy(d, s, k):
         send = (z + nz - s) % nz if d == 0 else (z + s) % nz
@@ -141,11 +144,11 @@
     lax.fori_loop(0, nz - 1, drain, 0)
 
 
-def grid_allreduce(x, cid, shape=None, flags=None):
+def grid_allreduce(x, cid, shape=None, flags=None, extra=()):
     shape = x.shape if shape is None else shape
     _, nz, m, rows, cols = shape
-    ins = (x,) if flags is None else (flags, x)
-    specs = [pl.BlockSpec(memory_space=pltpu.VMEM)]
+    ins = (x,) + tuple(extra) if flags is None else (flags, x) + tuple(extra)
+    specs = [pl.BlockSpec(memory_space=pltpu.VMEM)] * (1 + len(extra))
     if flags is not None:
         specs = [pl.BlockSpec(memory_space=pltpu.SMEM)] + specs
     return pl.pallas_call(
@@ -295,14 +298,14 @@
         steps = owner_steps.shape[0]
         is_mine = owner_steps == device
         covered = jnp.any(is_mine)
-        kv = jnp.concatenate([key_states, value_states], axis=1)
         nz = n // 2
         sub = 16
         m = steps * tokens // (2 * nz * sub)
         per = 2 * nz // steps
         kv_all = grid_allreduce(
-            kv.reshape(per, m, sub, 2 * features), 0,
+            key_states.reshape(per, m, sub, features), 0,
             shape=(2, nz, m, sub, 2 * features), flags=is_mine.astype(jnp.int32),
+            extra=(value_states.reshape(per, m, sub, features),),
         ).reshape(steps, tokens, 2 * features)
         listed = jnp.any(block_routes[0][None, :] == owner_steps[:, None], axis=1)
         remote = listed & (owner_steps != device) & (owner_steps < device)

time: 196 us -> 194 us (0.990)
  no operation moved by 1% of the time
where the time goes in v13:
time: 194 us
  Pallas kernels  184 us (95%)
  other arithmetic  7.52 us (4%)
  between operations  2.77 us (1%)
    pallas_call x2, Pallas kernels, grid_allreduce(): pl.pallas_call(functools.partial(grid_kernel, nz, m, len(ins)), out_shape...  154 us
    pallas_call x1, Pallas kernels, pair_terms(): pl.pallas_call(functools.partial(pair_kernel, scale, group), out_shape=(j...  29.6 us

profile of v13, /device:TPU:6, one launch (start us, length us, event | category | flops | bytes accessed | tf_op | source)
XLA Modules:
  0.0 193.9 jit_solution(5460014929703459716)
XLA Ops:
  0.6 0.9 compare_reduce_fusion
  1.5 1.8 fusion.2
  3.3 0.6 add_convert_fusion.flag_ref
  3.9 1.4 iota_reduce_fusion
  7.3 69.3 %shard_map.103 = bf16[2,8,4,16,1024]{4,3,2,1,0:T(8,128)(2,1)} custom-call(s32[4]{0:T(128)} %get-tuple-element.16.refs_0_, bf16[4,4,16,512]{3,2,1,0:T(8,128)(2,1)} %bitcast.11, bf16[4,4,16,512]{3,2,1,0:T(8,128)(2,1)} %bitcast.12), custom_call_target="tpu_custom_call" | custom-call | tf_op jit(solution)/shard_map/pallas_call | solution.py:154
  76.7 29.6 %shard_map.104 = (bf16[256,2048]{1,0:T(8,128)(2,1)}, f32[256,512]{1,0:T(8,128)}, f32[256,512]{1,0:T(8,128)}, f32[4,256,1024]{2,1,0:T(8,128)}) custom-call(s32[5]{0:T(128)} %add_convert_fusion.flag_ref, bf16[256,2048]{1,0:T(8,128)(2,1)} %q_ref.1, bf16[256,2048]{1,0:T(8,128)(2,1)} %do_ref.1, bf16[256,512]{1,0:T(8,128)(2,1)} %k_ref.1, bf16[256,512]{1,0:T(8,128)(2,1)} %v_ref.1, ...), custom_call_target="tpu_custom_call" | custom-call | tf_op jit(solution)/shard_map/pallas_call | solution.py:245
  106.3 0.0 copy-start
  106.3 0.0 copy-start.1
  106.3 84.7 %shard_map.105 = f32[2,8,8,8,1024]{4,3,2,1,0:T(8,128)} custom-call(f32[2,8,8,8,1024]{4,3,2,1,0:T(8,128)} %bitcast.10), custom_call_target="tpu_custom_call" | custom-call | tf_op jit(solution)/shard_map/pallas_call | solution.py:154
  191.0 1.9 %select_bitcast_fusion = f32[256,1024]{1,0:T(8,128)S(1)} fusion(f32[4,256,1024]{2,1,0:T(8,128)} %bitcast.9, s32[]{:T(128)S(6)} %select_n.20, pred[]{:T(512)} %get-tuple-element.15), kind=kLoop, calls=%fused_computation | loop fusion | flops 262144 | bytes 2097157 | tf_op jit(solution)/shard_map/jit(_where)/select_n | solution.py:318
  192.9 0.0 copy-done
  193.0 0.0 copy-done.1
  193.0 0.9 fusion
Async XLA Ops:
  106.3 86.7 %copy-start = (f32[256,512]{1,0:T(8,128)S(1)}, f32[256,512]{1,0:T(8,128)}, u32[]{:S(2)}) copy-start(f32[256,512]{1,0:T(8,128)} %get-tuple-element.9) | copy-start | bytes 1572868
  106.3 86.7 %copy-start.1 = (f32[256,512]{1,0:T(8,128)S(1)}, f32[256,512]{1,0:T(8,128)}, u32[]{:S(2)}) copy-start(f32[256,512]{1,0:T(8,128)} %get-tuple-element.12) | copy-start | bytes 1572868

commit v14 on v13

--- a/solution.py
+++ b/solution.py
@@ -314,7 +314,8 @@
             flags, queries, grad_output, log_norms, grad_dots, key_states, value_states, kv_all
         )
         summed = slot_allreduce(terms, n, 1)
-        held = lax.dynamic_index_in_dim(summed, jnp.argmax(is_mine), keepdims=False)
+        owned = jnp.sum(jnp.where(is_mine, jnp.arange(steps, dtype=jnp.int32), 0))
+        held = lax.dynamic_index_in_dim(summed, owned, keepdims=False)
         held = jnp.where(covered, held, jnp.float32(0.0))
         grad_k = grad_k + held[:, :features]
         grad_v = grad_v + held[:, features:]

time: 194 us -> 194 us (level)
  no operation moved by 1% of the time
where the time goes in v14:
time: 194 us
  Pallas kernels  183 us (94%)
  other arithmetic  7.43 us (4%)
  between operations  2.63 us (1%)
    pallas_call x2, Pallas kernels, grid_allreduce(): pl.pallas_call(functools.partial(grid_kernel, nz, m, len(ins)), out_shape...  154 us
    pallas_call x1, Pallas kernels, pair_terms(): pl.pallas_call(functools.partial(pair_kernel, scale, group), out_shape=(j...  29.6 us

profile of v14, /device:TPU:6, one launch (start us, length us, event | category | flops | bytes accessed | tf_op | source)
XLA Modules:
  0.0 193.5 jit_solution(13281381923378081700)
XLA Ops:
  0.6 1.3 select_reduce_fusion
  3.9 0.9 compare_reduce_fusion
  4.7 1.8 fusion.2
  6.5 0.6 add_convert_fusion.flag_ref
  7.1 69.2 %shard_map.103 = bf16[2,8,4,16,1024]{4,3,2,1,0:T(8,128)(2,1)} custom-call(s32[4]{0:T(128)} %get-tuple-element.14.refs_0_, bf16[4,4,16,512]{3,2,1,0:T(8,128)(2,1)} %bitcast.11, bf16[4,4,16,512]{3,2,1,0:T(8,128)(2,1)} %bitcast.12), custom_call_target="tpu_custom_call" | custom-call | tf_op jit(solution)/shard_map/pallas_call | solution.py:154
  76.3 29.6 %shard_map.104 = (bf16[256,2048]{1,0:T(8,128)(2,1)}, f32[256,512]{1,0:T(8,128)}, f32[256,512]{1,0:T(8,128)}, f32[4,256,1024]{2,1,0:T(8,128)}) custom-call(s32[5]{0:T(128)} %add_convert_fusion.flag_ref, bf16[256,2048]{1,0:T(8,128)(2,1)} %q_ref.1, bf16[256,2048]{1,0:T(8,128)(2,1)} %do_ref.1, bf16[256,512]{1,0:T(8,128)(2,1)} %k_ref.1, bf16[256,512]{1,0:T(8,128)(2,1)} %v_ref.1, ...), custom_call_target="tpu_custom_call" | custom-call | tf_op jit(solution)/shard_map/pallas_call | solution.py:245
  105.9 0.0 copy-start
  105.9 0.0 copy-start.1
  105.9 84.7 %shard_map.105 = f32[2,8,8,8,1024]{4,3,2,1,0:T(8,128)} custom-call(f32[2,8,8,8,1024]{4,3,2,1,0:T(8,128)} %bitcast.10), custom_call_target="tpu_custom_call" | custom-call | tf_op jit(solution)/shard_map/pallas_call | solution.py:154
  190.6 1.9 %select_bitcast_fusion = f32[256,1024]{1,0:T(8,128)S(1)} fusion(f32[4,256,1024]{2,1,0:T(8,128)} %bitcast.9, s32[]{:T(128)S(6)} %select_n.21, pred[]{:T(512)} %get-tuple-element.13), kind=kLoop, calls=%fused_computation | loop fusion | flops 262144 | bytes 2097157 | tf_op jit(solution)/shard_map/jit(_where)/select_n | solution.py:319
  192.6 0.0 copy-done
  192.6 0.0 copy-done.1
  192.6 0.9 fusion
Async XLA Ops:
  105.9 86.7 %copy-start = (f32[256,512]{1,0:T(8,128)S(1)}, f32[256,512]{1,0:T(8,128)}, u32[]{:S(2)}) copy-start(f32[256,512]{1,0:T(8,128)} %get-tuple-element.8) | copy-start | bytes 1572868
  105.9 86.7 %copy-start.1 = (f32[256,512]{1,0:T(8,128)S(1)}, f32[256,512]{1,0:T(8,128)}, u32[]{:S(2)}) copy-start(f32[256,512]{1,0:T(8,128)} %get-tuple-element.10) | copy-start | bytes 1572868
